TPU v7x, 128 devices: a whole 4x4x4 slice. The times are simulated.
128 devices in a mesh: section: 4 (over x_lo, core), seq: 8 (over x_hi, z), tp: 4 (over y).
Axes of the slice: x: 4 (x_hi: 2, x_lo: 2; x = x_hi * 2 + x_lo), y: 4, z: 4, core: 2. Of those that a mesh axis runs over, the one named last changes fastest.
Arguments:
- streams: float32 [4, 4, 1024, 1280], P('section', None, 'seq'), may hold values from -6 to 6
- head_streams: float32 [4, 1024, 1280], P(None, 'seq'), may hold values from -6 to 6
- gains: float32 [4, 2, 1280], P('section'), may hold values from 0.1 to 1.9
- w_qkv: bfloat16 [4, 1280, 3, 1280], P('section', None, None, 'tp'), may hold values from -40 to 40
- w_out: bfloat16 [4, 1280, 1280], P('section', None, 'tp'), may hold values from -0.15625 to 0.15625
- w_up: bfloat16 [4, 1280, 5120], P('section', None, 'tp'), may hold values from -0.15625 to 0.15625
- w_down: bfloat16 [4, 1280, 5120], P('section', None, 'tp'), may hold values from -0.078125 to 0.078125
Outputs:
- recon: float32 [4, 4, 1024, 1280], P('section', None, 'seq')
- grad_qkv: bfloat16 [4, 1280, 3, 1280], P('section', 'seq', None, 'tp')
- grad_out: bfloat16 [4, 1280, 1280], P('section', 'seq', 'tp')
- grad_up: bfloat16 [4, 1280, 5120], P('section', 'seq', 'tp')
- grad_down: bfloat16 [4, 1280, 5120], P('section', 'seq', 'tp')
All inputs are finite; a program needn't handle non-finite values.
Results may differ from a plain program's by a relative error of at most 0.028.
Values may be sent and summed in bfloat16 or wider, within the bound.
A program may use at most 128 MiB of HBM per device.

v0:
```python
import jax
import jax.numpy as jnp
from jax import lax
from jax.sharding import Mesh
from jax.sharding import PartitionSpec as P

HEAD_DIM = 64
TICKS = 2
SEQ = ("seq_0", "seq_1")


def copy_for_each(shard, axis):
    copies = jnp.broadcast_to(shard, (lax.axis_size(axis), *shard.shape))
    return lax.all_to_all(copies, axis, split_axis=0, concat_axis=0, tiled=True)


def over_copies(shard, axis):
    return copy_for_each(shard, axis).sum(axis=0)


def laid_out(tiles, dim):
    tiles = jnp.moveaxis(tiles, 0, dim)
    shape = tiles.shape
    return tiles.reshape(*shape[:dim], shape[dim] * shape[dim + 1], *shape[dim + 2 :])


def gather_directly(shard, axis, dim):
    return laid_out(copy_for_each(shard, axis), dim)


def taken_together(shard, axis):
    everything = copy_for_each(shard, axis)
    return jnp.sum(everything.astype(jnp.float32), axis=0)


def in_blocks(shard, dim, length):
    before, after = (shard.shape[:dim], shard.shape[dim + 1 :])
    return jnp.moveaxis(shard.reshape(*before, length, -1, *after), dim, 0)


def sent_and_summed(shard, axis, dim):
    length = lax.axis_size(axis)
    tiles = lax.all_to_all(in_blocks(shard, dim, length), axis, 0, 0, tiled=True)
    return jnp.sum(tiles.astype(jnp.float32), axis=0)


def from_behind(shard, axis, by):
    length = lax.axis_size(axis)
    pairs = [(i, i + by) for i in range(length) if 0 <= i + by < length]
    return lax.ppermute(shard, axis, pairs)


def as_sent(shard):
    return jax.tree.map(lambda a: a.astype(jnp.bfloat16) if a.dtype == jnp.float32 else a, shard)


def own_block(tiles, axes, order):
    inside = tiles.shape[1:]
    tiles = tiles.reshape(*(lax.axis_size(a) for a in axes), *inside)
    tiles = jnp.moveaxis(tiles, order, range(len(axes))).reshape(-1, *inside)
    for k in order:
        tiles = lax.psum_scatter(tiles, axes[k], scatter_dimension=0, tiled=True)
    return tiles[0]


def summed_rows(shard, axes, order, dim):
    length = lax.axis_size(axes)
    return own_block(in_blocks(shard, dim, length), axes, order)


def layer_norm(values, gain):
    centre = values - jnp.mean(values, -1, keepdims=True)
    inv_std = lax.rsqrt(jnp.mean(centre * centre, -1, keepdims=True) + 1e-06)
    unit_vals = centre * inv_std
    return (unit_vals * gain, unit_vals, inv_std)


def norm_back(grad, gain, unit_vals, inv_std):
    scaled = grad * gain
    return inv_std * (
        scaled
        - jnp.mean(scaled, -1, keepdims=True)
        - unit_vals * jnp.mean(scaled * unit_vals, -1, keepdims=True)
    )


def gelu_tanh(values):
    return jax.nn.gelu(values, approximate=True)


def block_step(inputs, gain_pair, w_flat, w_out, w_up, w_down):
    upper, lower, grad_upper, grad_lower = (inputs[0], inputs[1], inputs[2], inputs[3])
    rows = upper.shape[0]
    local = w_out.shape[1]
    heads = local // HEAD_DIM
    normed_up, unit_up, inv_up = layer_norm(upper, gain_pair[1])
    normed_low = normed_up.astype(jnp.bfloat16)
    hidden_pre = jnp.dot(normed_low, w_up, preferred_element_type=jnp.float32)
    hidden = gelu_tanh(hidden_pre).astype(jnp.bfloat16)
    mlp_part = jnp.einsum("tf,df->td", hidden, w_down, preferred_element_type=jnp.float32)
    grad_lower_low = grad_lower.astype(jnp.bfloat16)
    grad_hidden = jnp.dot(grad_lower_low, w_down, preferred_element_type=jnp.float32)
    unused, pull = jax.vjp(gelu_tanh, hidden_pre)
    grad_pre = pull(grad_hidden)[0].astype(jnp.bfloat16)
    normed_part = jnp.einsum("tf,df->td", grad_pre, w_up, preferred_element_type=jnp.float32)
    mlp_out = over_copies(mlp_part, "tp")
    lower_in = lower - mlp_out
    normed_att, unit_att, inv_att = layer_norm(lower_in, gain_pair[0])
    att_low = normed_att.astype(jnp.bfloat16)
    projected = (
        jnp.dot(att_low, w_flat, preferred_element_type=jnp.float32)
        .astype(jnp.bfloat16)
        .reshape(rows, 3, local)
    )
    query = projected[:, 0]
    key_value = projected[:, 1:]
    gathered = gather_directly(key_value, SEQ, 0)
    query_heads = query.reshape(rows, heads, HEAD_DIM)
    all_keys = gathered[:, 0].reshape(-1, heads, HEAD_DIM)
    all_values = gathered[:, 1].reshape(-1, heads, HEAD_DIM)
    scores = (
        jnp.einsum("qhd,khd->hqk", query_heads, all_keys, preferred_element_type=jnp.float32)
        * 0.125
    )
    top = jnp.max(scores, -1, keepdims=True)
    lse = top + jnp.log(jnp.sum(jnp.exp(scores - top), -1, keepdims=True))
    probs = jnp.exp(scores - lse)
    probs_low = probs.astype(jnp.bfloat16)
    mixed = (
        jnp.einsum("hqk,khd->qhd", probs_low, all_values, preferred_element_type=jnp.float32)
        .astype(jnp.bfloat16)
        .reshape(rows, local)
    )
    att_part = jnp.einsum("tc,dc->td", mixed, w_out, preferred_element_type=jnp.float32)
    att_out = taken_together(att_part.astype(jnp.bfloat16), "tp").astype(jnp.float32)
    grad_normed = taken_together(normed_part.astype(jnp.bfloat16), "tp").astype(jnp.float32)
    upper_total = grad_upper + norm_back(grad_normed, gain_pair[1], unit_up, inv_up)
    total_low = upper_total.astype(jnp.bfloat16)
    grad_mixed = jnp.dot(total_low, w_out, preferred_element_type=jnp.float32).astype(jnp.bfloat16)
    grad_heads = grad_mixed.reshape(rows, heads, HEAD_DIM)
    grad_probs = jnp.einsum(
        "qhd,khd->hqk", grad_heads, all_values, preferred_element_type=jnp.float32
    )
    delta = jnp.sum(probs * grad_probs, -1, keepdims=True)
    grad_scores = (probs * (grad_probs - delta)).astype(jnp.bfloat16)
    grad_query = (
        (
            0.125
            * jnp.einsum("hqk,khd->qhd", grad_scores, all_keys, preferred_element_type=jnp.float32)
        )
        .astype(jnp.bfloat16)
        .reshape(rows, local)
    )
    grad_keys = 0.125 * jnp.einsum(
        "hqk,qhd->khd", grad_scores, query_heads, preferred_element_type=jnp.float32
    )
    grad_values = jnp.einsum(
        "hqk,qhd->khd", probs_low, grad_heads, preferred_element_type=jnp.float32
    )
    kv_grad = sent_and_summed(
        jnp.stack(
            [
                grad_keys.reshape(rows * lax.axis_size(SEQ), local),
                grad_values.reshape(rows * lax.axis_size(SEQ), local),
            ],
            1,
        ).astype(jnp.bfloat16),
        SEQ,
        0,
    ).astype(jnp.bfloat16)
    grad_proj = jnp.concatenate([grad_query[:, None], kv_grad], 1).reshape(rows, 3 * local)
    att_grad_part = jnp.einsum("tc,dc->td", grad_proj, w_flat, preferred_element_type=jnp.float32)
    grad_att = taken_together(att_grad_part.astype(jnp.bfloat16), "tp").astype(jnp.float32)
    upper_in = upper - att_out
    grad_lower_in = grad_lower + norm_back(grad_att, gain_pair[0], unit_att, inv_att)
    result = jnp.stack([upper_in, lower_in, upper_total, grad_lower_in])
    terms = (
        jnp.dot(att_low.T, grad_proj, preferred_element_type=jnp.float32),
        jnp.dot(total_low.T, mixed, preferred_element_type=jnp.float32),
        jnp.dot(normed_low.T, grad_pre, preferred_element_type=jnp.float32),
        jnp.dot(grad_lower_low.T, hidden, preferred_element_type=jnp.float32),
    )
    return (result, terms)


def per_device(streams, head_streams, gains, w_qkv, w_out, w_up, w_down):
    gain_pair = gains[0]
    width = w_qkv.shape[1]
    local = w_qkv.shape[3]
    w_flat = w_qkv[0].reshape(width, 3 * local)
    inputs = streams[0]
    totals = None
    result = None
    for tick in range(TICKS):
        if tick > 0:
            received = from_behind(result.astype(jnp.bfloat16), "section", -1).astype(result.dtype)
            is_last = lax.axis_index("section") == lax.axis_size("section") - 1
            inputs = jnp.where(is_last, head_streams, received)
        result, terms = block_step(inputs, gain_pair, w_flat, w_out[0], w_up[0], w_down[0])
        totals = terms if totals is None else tuple((old + new for old, new in zip(totals, terms)))
    grad_qkv, grad_out, grad_up, grad_down = jax.tree.map(
        lambda part: part.astype(jnp.float32),
        jax.tree.map(lambda part: summed_rows(part, SEQ, (1, 0), 0), as_sent(totals)),
    )
    grad_qkv = grad_qkv.astype(jnp.bfloat16).reshape(-1, 3, local)[None]
    return (
        result[None],
        grad_qkv,
        grad_out.astype(jnp.bfloat16)[None],
        grad_up.astype(jnp.bfloat16)[None],
        grad_down.astype(jnp.bfloat16)[None],
    )


def solution(mesh):
    torus = Mesh(
        mesh.devices.reshape(mesh.shape["section"], 2, 4, mesh.shape["tp"]),
        ("section", "seq_0", "seq_1", "tp"),
    )
    placed = (
        P("section", None, SEQ, None),
        P(None, SEQ, None),
        P("section", None, None),
        P("section", None, None, "tp"),
        P("section", None, "tp"),
        P("section", None, "tp"),
        P("section", None, "tp"),
    )
    return jax.shard_map(
        per_device,
        mesh=torus,
        in_specs=placed,
        out_specs=(
            P("section", None, SEQ, None),
            P("section", SEQ, None, "tp"),
            P("section", SEQ, "tp"),
            P("section", SEQ, "tp"),
            P("section", SEQ, "tp"),
        ),
        check_vma=False,
    )
```

profile of v0, /device:TPU:1, one launch (start us, length us, event | category | flops | bytes accessed | tf_op | source)
XLA Modules:
  0.0 577.5 jit_solution(15459344806008210653)
XLA Ops:
  18.5 5.0 all-to-all-start.3
  27.6 13.1 %all-to-all-done.3 = bf16[4,128,1280]{2,1,0:T(8,128)(2,1)} async-done(((bf16[4,128,1280]{2,1,0:T(8,128)(2,1)}), bf16[4,128,1280]{2,1,0:T(8,128)(2,1)}, u32[]{:S(2)}, u32[]{:S(2)}) %all-to-all-start.3) | async-done | bytes 1310752 | tf_op jit(solution)/shard_map/all_to_all | solution.py:14
  43.5 4.5 all-to-all-start
  50.4 27.9 %all-to-all-done = f32[4,128,1280]{2,1,0:T(8,128)} async-done(((f32[4,128,1280]{2,1,0:T(8,128)}), f32[4,128,1280]{2,1,0:T(8,128)}, u32[]{:S(2)}, u32[]{:S(2)}) %all-to-all-start) | async-done | bytes 2621472 | tf_op jit(solution)/shard_map/all_to_all | solution.py:14
  88.8 7.6 %all-to-all-start.1 = ((bf16[8,128,2,320]{1,3,2,0:T(8,128)(2,1)}), bf16[8,128,2,320]{1,3,2,0:T(8,128)(2,1)}, u32[]{:S(2)}, u32[]{:S(2)}) async-start(bf16[8,128,2,320]{1,3,2,0:T(8,128)(2,1)} %broadcast_in_dim.23), calls=%async_computation.1 | async-start | bytes 2621440 | tf_op jit(solution)/shard_map/all_to_all | solution.py:14
  98.7 13.0 %all-to-all-done.1 = bf16[8,128,2,320]{1,3,2,0:T(8,128)(2,1)} async-done(((bf16[8,128,2,320]{1,3,2,0:T(8,128)(2,1)}), bf16[8,128,2,320]{1,3,2,0:T(8,128)(2,1)}, u32[]{:S(2)}, u32[]{:S(2)}) %all-to-all-start.1) | async-done | bytes 1310752 | tf_op jit(solution)/shard_map/all_to_all | solution.py:14
  120.5 7.6 %all-to-all-start.4 = ((bf16[8,128,2,320]{1,3,2,0:T(8,128)(2,1)}), bf16[8,128,2,320]{1,3,2,0:T(8,128)(2,1)}, u32[]{:S(2)}, u32[]{:S(2)}) async-start(bf16[8,128,2,320]{1,3,2,0:T(8,128)(2,1)} %pad_maximum_fusion), calls=%async_computation.4 | async-start | bytes 2621440 | tf_op jit(solution)/shard_map/all_to_all | solution.py:43
  132.6 12.7 %all-to-all-done.4 = bf16[8,128,2,320]{1,3,2,0:T(8,128)(2,1)} async-done(((bf16[8,128,2,320]{1,3,2,0:T(8,128)(2,1)}), bf16[8,128,2,320]{1,3,2,0:T(8,128)(2,1)}, u32[]{:S(2)}, u32[]{:S(2)}) %all-to-all-start.4) | async-done | bytes 1310752 | tf_op jit(solution)/shard_map/all_to_all | solution.py:43
  147.5 4.7 all-to-all-start.2
  161.1 7.3 %all-to-all-done.2 = bf16[4,128,1280]{2,1,0:T(8,128)(2,1)} async-done(((bf16[4,128,1280]{2,1,0:T(8,128)(2,1)}), bf16[4,128,1280]{2,1,0:T(8,128)(2,1)}, u32[]{:S(2)}, u32[]{:S(2)}) %all-to-all-start.2) | async-done | bytes 1310752 | tf_op jit(solution)/shard_map/all_to_all | solution.py:14
  170.5 4.3 all-to-all-start.5
  179.7 10.5 %all-to-all-done.5 = bf16[4,128,1280]{2,1,0:T(8,128)(2,1)} async-done(((bf16[4,128,1280]{2,1,0:T(8,128)(2,1)}), bf16[4,128,1280]{2,1,0:T(8,128)(2,1)}, u32[]{:S(2)}, u32[]{:S(2)}) %all-to-all-start.5) | async-done | bytes 1310752 | tf_op jit(solution)/shard_map/all_to_all | solution.py:14
  195.8 5.5 collective-permute-start
  201.2 15.8 %collective-permute-done = bf16[4,128,1280]{2,1,0:T(8,128)(2,1)} collective-permute-done((bf16[4,128,1280]{2,1,0:T(8,128)(2,1)}, bf16[4,128,1280]{2,1,0:T(8,128)(2,1)}, u32[]{:S(2)}, u32[]{:S(2)}) %collective-permute-start) | collective-permute-done | bytes 1310752 | tf_op jit(solution)/shard_map/ppermute | solution.py:50
  225.7 4.4 all-to-all-start.9
  233.2 8.1 %all-to-all-done.9 = bf16[4,128,1280]{2,1,0:T(8,128)(2,1)} async-done(((bf16[4,128,1280]{2,1,0:T(8,128)(2,1)}), bf16[4,128,1280]{2,1,0:T(8,128)(2,1)}, u32[]{:S(2)}, u32[]{:S(2)}) %all-to-all-start.9) | async-done | bytes 1310752 | tf_op jit(solution)/shard_map/all_to_all | solution.py:14
  244.1 4.5 all-to-all-start.6
  251.2 18.9 %all-to-all-done.6 = f32[4,128,1280]{2,1,0:T(8,128)} async-done(((f32[4,128,1280]{2,1,0:T(8,128)}), f32[4,128,1280]{2,1,0:T(8,128)}, u32[]{:S(2)}, u32[]{:S(2)}) %all-to-all-start.6) | async-done | bytes 2621472 | tf_op jit(solution)/shard_map/all_to_all | solution.py:14
  278.7 7.5 %all-to-all-start.7 = ((bf16[8,128,2,320]{1,3,2,0:T(8,128)(2,1)}), bf16[8,128,2,320]{1,3,2,0:T(8,128)(2,1)}, u32[]{:S(2)}, u32[]{:S(2)}) async-start(bf16[8,128,2,320]{1,3,2,0:T(8,128)(2,1)} %broadcast_in_dim.28), calls=%async_computation.7 | async-start | bytes 2621440 | tf_op jit(solution)/shard_map/all_to_all | solution.py:14
  287.8 10.2 %all-to-all-done.7 = bf16[8,128,2,320]{1,3,2,0:T(8,128)(2,1)} async-done(((bf16[8,128,2,320]{1,3,2,0:T(8,128)(2,1)}), bf16[8,128,2,320]{1,3,2,0:T(8,128)(2,1)}, u32[]{:S(2)}, u32[]{:S(2)}) %all-to-all-start.7) | async-done | bytes 1310752 | tf_op jit(solution)/shard_map/all_to_all | solution.py:14
  316.7 6.4 %all-to-all-done.10 = bf16[8,128,2,320]{1,3,2,0:T(8,128)(2,1)} async-done(((bf16[8,128,2,320]{1,3,2,0:T(8,128)(2,1)}), bf16[8,128,2,320]{1,3,2,0:T(8,128)(2,1)}, u32[]{:S(2)}, u32[]{:S(2)}) %all-to-all-start.10) | async-done | bytes 1310752 | tf_op jit(solution)/shard_map/all_to_all | solution.py:43
  326.3 4.8 add_convert_fusion
  331.1 4.4 copy.60
  356.4 16.4 %reduce-scatter.9.cloned.1.call-done = bf16[2,160,960]{2,1,0:T(8,128)(2,1)} async-done(((bf16[8,160,960]{2,1,0:T(8,128)(2,1)}), bf16[2,160,960]{2,1,0:T(8,128)(2,1)}) %reduce-scatter.9.cloned.1.call-update) | async-done | bytes 614416 | tf_op jit(solution)/shard_map/reduce_scatter | solution.py:62
  372.9 24.9 %reduce-scatter.13.cloned.1.call-done = bf16[2,160,320]{2,1,0:T(8,128)(2,1)} async-done(((bf16[8,160,320]{2,1,0:T(8,128)(2,1)}), bf16[2,160,320]{2,1,0:T(8,128)(2,1)}) %reduce-scatter.13.cloned.1.call-update) | async-done | bytes 204816 | tf_op jit(solution)/shard_map/reduce_scatter | solution.py:62
  400.5 4.3 all-to-all-start.8
  404.9 35.8 %reduce-scatter.21.cloned.1.call-done = bf16[2,160,1280]{2,1,0:T(8,128)(2,1)} async-done(((bf16[8,160,1280]{2,1,0:T(8,128)(2,1)}), bf16[2,160,1280]{2,1,0:T(8,128)(2,1)}) %reduce-scatter.21.cloned.1.call-update) | async-done | bytes 819216 | tf_op jit(solution)/shard_map/reduce_scatter | solution.py:62
  452.6 29.5 %reduce-scatter.17.cloned.1.call-done = bf16[2,160,1280]{2,1,0:T(8,128)(2,1)} async-done(((bf16[8,160,1280]{2,1,0:T(8,128)(2,1)}), bf16[2,160,1280]{2,1,0:T(8,128)(2,1)}) %reduce-scatter.17.cloned.1.call-update) | async-done | bytes 819216 | tf_op jit(solution)/shard_map/reduce_scatter | solution.py:62
  489.5 14.4 %reduce-scatter.11.cloned.1.call-done = bf16[1,160,960]{2,1,0:T(8,128)(2,1)} async-done(((bf16[2,160,960]{2,1,0:T(8,128)(2,1)}), bf16[1,160,960]{2,1,0:T(8,128)(2,1)}) %reduce-scatter.11.cloned.1.call-update) | async-done | bytes 307216 | tf_op jit(solution)/shard_map/reduce_scatter | solution.py:62
  507.9 13.9 %reduce-scatter.15.cloned.1.call-done = bf16[1,160,320]{2,1,0:T(8,128)(2,1)} async-done(((bf16[2,160,320]{2,1,0:T(8,128)(2,1)}), bf16[1,160,320]{2,1,0:T(8,128)(2,1)}) %reduce-scatter.15.cloned.1.call-update) | async-done | bytes 102416 | tf_op jit(solution)/shard_map/reduce_scatter | solution.py:62
  521.8 24.3 %reduce-scatter.23.cloned.1.call-done = bf16[1,160,1280]{2,1,0:T(8,128)(2,1)} async-done(((bf16[2,160,1280]{2,1,0:T(8,128)(2,1)}), bf16[1,160,1280]{2,1,0:T(8,128)(2,1)}) %reduce-scatter.23.cloned.1.call-update) | async-done | bytes 409616 | tf_op jit(solution)/shard_map/reduce_scatter | solution.py:62
  546.1 24.3 %reduce-scatter.19.cloned.1.call-done = bf16[1,160,1280]{2,1,0:T(8,128)(2,1)} async-done(((bf16[2,160,1280]{2,1,0:T(8,128)(2,1)}), bf16[1,160,1280]{2,1,0:T(8,128)(2,1)}) %reduce-scatter.19.cloned.1.call-update) | async-done | bytes 409616 | tf_op jit(solution)/shard_map/reduce_scatter | solution.py:62
  (258 shorter events, 165.2 us)
Async XLA Ops:
  8.5 4.9 copy-start.16
  18.5 22.2 %all-to-all-start.3 = ((bf16[4,128,1280]{2,1,0:T(8,128)(2,1)}), bf16[4,128,1280]{2,1,0:T(8,128)(2,1)}, u32[]{:S(2)}, u32[]{:S(2)}) async-start(bf16[4,128,1280]{2,1,0:T(8,128)(2,1)} %broadcast_in_dim.25), calls=%async_computation.3 | async-start | bytes 2621440 | tf_op jit(solution)/shard_map/all_to_all | solution.py:14
  43.5 34.9 %all-to-all-start = ((f32[4,128,1280]{2,1,0:T(8,128)}), f32[4,128,1280]{2,1,0:T(8,128)}, u32[]{:S(2)}, u32[]{:S(2)}) async-start(f32[4,128,1280]{2,1,0:T(8,128)} %broadcast_in_dim.22), calls=%async_computation | async-start | bytes 5242880 | tf_op jit(solution)/shard_map/all_to_all | solution.py:14
  88.8 22.8 %all-to-all-start.1 = ((bf16[8,128,2,320]{1,3,2,0:T(8,128)(2,1)}), bf16[8,128,2,320]{1,3,2,0:T(8,128)(2,1)}, u32[]{:S(2)}, u32[]{:S(2)}) async-start(bf16[8,128,2,320]{1,3,2,0:T(8,128)(2,1)} %broadcast_in_dim.23), calls=%async_computation.1 | async-start | bytes 2621440 | tf_op jit(solution)/shard_map/all_to_all | solution.py:14
  98.7 15.4 %copy-start.44 = (bf16[128,1,320]{0,2,1:T(8,128)(2,1)S(1)}, bf16[128,1,320]{0,2,1:T(8,128)(2,1)}, u32[]{:S(2)}) copy-start(bf16[128,1,320]{0,2,1:T(8,128)(2,1)} %slice.86) | copy-start | bytes 245764
  120.5 24.8 %all-to-all-start.4 = ((bf16[8,128,2,320]{1,3,2,0:T(8,128)(2,1)}), bf16[8,128,2,320]{1,3,2,0:T(8,128)(2,1)}, u32[]{:S(2)}, u32[]{:S(2)}) async-start(bf16[8,128,2,320]{1,3,2,0:T(8,128)(2,1)} %pad_maximum_fusion), calls=%async_computation.4 | async-start | bytes 2621440 | tf_op jit(solution)/shard_map/all_to_all | solution.py:43
  147.5 20.9 %all-to-all-start.2 = ((bf16[4,128,1280]{2,1,0:T(8,128)(2,1)}), bf16[4,128,1280]{2,1,0:T(8,128)(2,1)}, u32[]{:S(2)}, u32[]{:S(2)}) async-start(bf16[4,128,1280]{2,1,0:T(8,128)(2,1)} %broadcast_in_dim.24), calls=%async_computation.2 | async-start | bytes 2621440 | tf_op jit(solution)/shard_map/all_to_all | solution.py:14
  170.5 19.7 %all-to-all-start.5 = ((bf16[4,128,1280]{2,1,0:T(8,128)(2,1)}), bf16[4,128,1280]{2,1,0:T(8,128)(2,1)}, u32[]{:S(2)}, u32[]{:S(2)}) async-start(bf16[4,128,1280]{2,1,0:T(8,128)(2,1)} %broadcast_in_dim.26), calls=%async_computation.5 | async-start | bytes 2621440 | tf_op jit(solution)/shard_map/all_to_all | solution.py:14
  174.8 17.1 %copy-start.55 = (f32[128]{0:T(128)S(1)}, f32[128]{0:T(128)}, u32[]{:S(2)}) copy-start(f32[128]{0:T(128)} %copy-done.54) | copy-start | bytes 1540
  195.8 21.3 %collective-permute-start = (bf16[4,128,1280]{2,1,0:T(8,128)(2,1)}, bf16[4,128,1280]{2,1,0:T(8,128)(2,1)}, u32[]{:S(2)}, u32[]{:S(2)}) collective-permute-start(bf16[4,128,1280]{2,1,0:T(8,128)(2,1)} %pad_maximum_fusion.1), channel_id=1, source_target_pairs={{32,0},{64,32},{96,64},{33,1},{65,33},{97,65},{34,2},{66,34},{98,6... | collective-permute-start | bytes 3932168 | tf_op jit(solution)/shard_map/ppermute | solution.py:50
  218.8 55.3 %copy-start.47 = (f32[128]{0:T(128)}, f32[128]{0:T(128)S(1)}, u32[]{:S(2)}) copy-start(f32[128]{0:T(128)S(1)} %broadcast_multiply_fusion.5) | copy-start | bytes 1540
  224.6 5.6 copy-start.18
  225.7 15.6 %all-to-all-start.9 = ((bf16[4,128,1280]{2,1,0:T(8,128)(2,1)}), bf16[4,128,1280]{2,1,0:T(8,128)(2,1)}, u32[]{:S(2)}, u32[]{:S(2)}) async-start(bf16[4,128,1280]{2,1,0:T(8,128)(2,1)} %broadcast_in_dim.30), calls=%async_computation.9 | async-start | bytes 2621440 | tf_op jit(solution)/shard_map/all_to_all | solution.py:14
  244.1 26.0 %all-to-all-start.6 = ((f32[4,128,1280]{2,1,0:T(8,128)}), f32[4,128,1280]{2,1,0:T(8,128)}, u32[]{:S(2)}, u32[]{:S(2)}) async-start(f32[4,128,1280]{2,1,0:T(8,128)} %broadcast_in_dim.27), calls=%async_computation.6 | async-start | bytes 5242880 | tf_op jit(solution)/shard_map/all_to_all | solution.py:14
  248.7 23.4 %copy-start.4 = (f32[4,128,1280]{2,1,0:T(8,128)S(1)}, f32[4,128,1280]{2,1,0:T(8,128)}, u32[]{:S(2)}) copy-start(f32[4,128,1280]{2,1,0:T(8,128)} %copy-done.3) | copy-start | bytes 7864324
  276.5 208.8 %copy-start.12 = (f32[1,128,1280]{2,1,0:T(8,128)}, f32[1,128,1280]{2,1,0:T(8,128)S(1)}, u32[]{:S(2)}) copy-start(f32[1,128,1280]{2,1,0:T(8,128)S(1)} %get-tuple-element.46) | copy-start | bytes 1966084
  277.4 9.5 %copy-start.15 = (bf16[1,1280,320]{1,2,0:T(8,128)(2,1)S(1)}, bf16[1,1280,320]{1,2,0:T(8,128)(2,1)}, u32[]{:S(2)}) copy-start(bf16[1,1280,320]{1,2,0:T(8,128)(2,1)} %param.11) | copy-start | bytes 2457604
  277.4 9.5 %copy-start.22 = (f32[1,128,1280]{2,1,0:T(8,128)S(1)}, f32[1,128,1280]{2,1,0:T(8,128)}, u32[]{:S(2)}) copy-start(f32[1,128,1280]{2,1,0:T(8,128)} %get-tuple-element.47) | copy-start | bytes 1966084
  278.7 19.3 %all-to-all-start.7 = ((bf16[8,128,2,320]{1,3,2,0:T(8,128)(2,1)}), bf16[8,128,2,320]{1,3,2,0:T(8,128)(2,1)}, u32[]{:S(2)}, u32[]{:S(2)}) async-start(bf16[8,128,2,320]{1,3,2,0:T(8,128)(2,1)} %broadcast_in_dim.28), calls=%async_computation.7 | async-start | bytes 2621440 | tf_op jit(solution)/shard_map/all_to_all | solution.py:14
  307.0 16.1 %all-to-all-start.10 = ((bf16[8,128,2,320]{1,3,2,0:T(8,128)(2,1)}), bf16[8,128,2,320]{1,3,2,0:T(8,128)(2,1)}, u32[]{:S(2)}, u32[]{:S(2)}) async-start(bf16[8,128,2,320]{1,3,2,0:T(8,128)(2,1)} %pad_maximum_fusion.2), calls=%async_computation.10 | async-start | bytes 2621440 | tf_op jit(solution)/shard_map/all_to_all | solution.py:43
  311.3 61.5 %reduce-scatter.9.cloned.1.call-start = ((), (), s32[]{:S(2)}) async-start(), calls=%async_computation.20 | async-start | bytes 3276800 | tf_op jit(solution)/shard_map/reduce_scatter | solution.py:62
  339.0 58.8 %reduce-scatter.13.cloned.1.call-start = ((), (), s32[]{:S(2)}) async-start(), calls=%async_computation.22 | async-start | bytes 1228800 | tf_op jit(solution)/shard_map/reduce_scatter | solution.py:62
  345.0 95.7 %reduce-scatter.21.cloned.1.call-start = ((), (), s32[]{:S(2)}) async-start(), calls=%async_computation.26 | async-start | bytes 4096000 | tf_op jit(solution)/shard_map/reduce_scatter | solution.py:62
  350.6 131.6 %reduce-scatter.17.cloned.1.call-start = ((), (), s32[]{:S(2)}) async-start(), calls=%async_computation.24 | async-start | bytes 4096000 | tf_op jit(solution)/shard_map/reduce_scatter | solution.py:62
  356.3 147.6 %reduce-scatter.11.cloned.1.call-start = ((), (), s32[]{:S(2)}) async-start(), calls=%async_computation.21 | async-start | bytes 983040 | tf_op jit(solution)/shard_map/reduce_scatter | solution.py:62
  372.8 149.0 %reduce-scatter.15.cloned.1.call-start = ((), (), s32[]{:S(2)}) async-start(), calls=%async_computation.23 | async-start | bytes 368640 | tf_op jit(solution)/shard_map/reduce_scatter | solution.py:62
  400.5 43.2 %all-to-all-start.8 = ((bf16[4,128,1280]{2,1,0:T(8,128)(2,1)}), bf16[4,128,1280]{2,1,0:T(8,128)(2,1)}, u32[]{:S(2)}, u32[]{:S(2)}) async-start(bf16[4,128,1280]{2,1,0:T(8,128)(2,1)} %broadcast_in_dim.29), calls=%async_computation.8 | async-start | bytes 2621440 | tf_op jit(solution)/shard_map/all_to_all | solution.py:14
  404.8 141.3 %reduce-scatter.23.cloned.1.call-start = ((), (), s32[]{:S(2)}) async-start(), calls=%async_computation.27 | async-start | bytes 1228800 | tf_op jit(solution)/shard_map/reduce_scatter | solution.py:62
  445.8 36.4 %all-to-all-start.11 = ((bf16[4,128,1280]{2,1,0:T(8,128)(2,1)}), bf16[4,128,1280]{2,1,0:T(8,128)(2,1)}, u32[]{:S(2)}, u32[]{:S(2)}) async-start(bf16[4,128,1280]{2,1,0:T(8,128)(2,1)} %broadcast_in_dim.31), calls=%async_computation.11 | async-start | bytes 2621440 | tf_op jit(solution)/shard_map/all_to_all | solution.py:14
  450.1 33.8 %copy-start.50 = (f32[128]{0:T(128)S(1)}, f32[128]{0:T(128)}, u32[]{:S(2)}) copy-start(f32[128]{0:T(128)} %copy-done.49) | copy-start | bytes 1540
  450.1 120.3 %reduce-scatter.19.cloned.1.call-start = ((), (), s32[]{:S(2)}) async-start(), calls=%async_computation.25 | async-start | bytes 1228800 | tf_op jit(solution)/shard_map/reduce_scatter | solution.py:62
  485.7 84.7 %copy-start.1 = (bf16[1,1280,1280]{2,1,0:T(8,128)(2,1)S(1)}, bf16[1,1280,1280]{2,1,0:T(8,128)(2,1)}, u32[]{:S(2)}) copy-start(bf16[1,1280,1280]{2,1,0:T(8,128)(2,1)} %param.12) | copy-start | bytes 9830404
  (47 other events, 107.4 us)
Sparse Core Ops, SparseCore 0:
  339.1 33.6 reduce-scatter.8
  375.8 21.9 reduce-scatter.12
  400.2 40.4 reduce-scatter.20
  443.0 39.1 reduce-scatter.16
  484.3 19.5 reduce-scatter.10
  506.7 15.0 reduce-scatter.14
  524.7 21.3 reduce-scatter.22
  549.0 21.3 reduce-scatter.18
where the time goes:
time: 588 us; the launch traced here: 577 us
  waiting for transfers between devices  328 us (56%)
  starting transfers between devices  69.1 us (12%)
  matrix products  58.8 us (10%)
  other arithmetic  53.5 us (9%)
  local copies, waits for them, and re-layouts  52.9 us (9%)
  between operations  15.5 us (3%)
    reduce_scatter x8, waiting for transfers between devices, own_block(): tiles = lax.psum_scatter(tiles, axes[k], scatter_dimension=0, tiled=True)  184 us
    all_to_all x10, waiting for transfers between devices, copy_for_each(): return lax.all_to_all(copies, axis, split_axis=0, concat_axis=0, tiled=True)  109 us
    all_to_all x10, starting transfers between devices, copy_for_each(): return lax.all_to_all(copies, axis, split_axis=0, concat_axis=0, tiled=True)  51.2 us
    all_to_all x2, waiting for transfers between devices, sent_and_summed(): lax.all_to_all(in_blocks(shard, dim, length), axis, 0, 0, tiled=True)  19.2 us
    broadcast_in_dim x10, local copies, waits for them, and re-layouts, copy_for_each(): copies = jnp.broadcast_to(shard, (lax.axis_size(axis), *shard.shape))  18 us
    ppermute x1, waiting for transfers between devices, from_behind(): return lax.ppermute(shard, axis, pairs)  15.8 us
    unnamed x121, local copies, waits for them, and re-layouts  13.7 us
    reduce_sum x6, other arithmetic, taken_together(): return jnp.sum(everything.astype(jnp.float32), axis=0)  13.2 us
  transfers between devices with their start and end apart: 21, of which 19 were waited for; matrix products, arithmetic and copies ran while one was open for 13% of the time, Pallas kernels for 0%

commit v1 on v0

v1 whole, which is shorter than its diff:
```python
import math

import jax
import jax.numpy as jnp
from jax import lax
from jax.experimental import pallas as pl
from jax.experimental.pallas import tpu as pltpu
from jax.sharding import PartitionSpec as P

MESH = pl.DeviceIdType.MESH
BF16 = jnp.bfloat16
F32 = jnp.float32
HEAD_DIM = 64
PAIR = 2 * HEAD_DIM
N_TP = 4
N_Z = 4
N_SEQ = 8
N_SEC = 4
NU, GL, AL, TL = 0, 1, 2, 3
NN = (((1,), (0,)), ((), ()))
NT = (((1,), (1,)), ((), ()))
TN = (((0,), (0,)), ((), ()))


def dot(a, b, dims):
    return lax.dot_general(a, b, dims, preferred_element_type=F32)


def loop(count, size, body):
    def step(i, carry):
        body(pl.multiple_of(i * size, size))
        return carry

    lax.fori_loop(0, count, step, 0)


def unit_of(values):
    centre = values - jnp.mean(values, -1, keepdims=True)
    inv_std = lax.rsqrt(jnp.mean(centre * centre, -1, keepdims=True) + 1e-06)
    return centre * inv_std, inv_std


def norm_back(grad, gain, values):
    unit, inv_std = unit_of(values)
    scaled = grad * gain
    return inv_std * (
        scaled
        - jnp.mean(scaled, -1, keepdims=True)
        - unit * jnp.mean(scaled * unit, -1, keepdims=True)
    )


GELU_C = math.sqrt(2.0 / math.pi)


def gelu(x):
    return 0.5 * x * (1.0 + jnp.tanh(GELU_C * (x + 0.044715 * (x * x * x))))


def gelu_slope(x):
    t = jnp.tanh(GELU_C * (x + 0.044715 * (x * x * x)))
    return 0.5 * (1.0 + t) + 0.5 * x * (1.0 - t * t) * (GELU_C * (1.0 + 0.134145 * (x * x)))


class Sender:
    def __init__(self, send_sem, recv_sem):
        self.send_sem, self.recv_sem = send_sem, recv_sem
        self.all = []

    def start(self, src, dst, device):
        k = len(self.all)
        copy = pltpu.make_async_remote_copy(
            src_ref=src,
            dst_ref=dst,
            send_sem=self.send_sem.at[k],
            recv_sem=self.recv_sem.at[k],
            device_id=device,
            device_id_type=MESH,
        )
        copy.start()
        self.all.append(copy)
        return copy


def received(copies):
    for copy in copies:
        copy.wait_recv()


def kernel(sizes, *refs):
    rows, width, hid, att, cut_mlp, cut_att = sizes
    (streams_h, head_h, gains_h, wkv_h, wqo_h, wup_h, wdn_h) = refs[:7]
    (recon_h, gatt_h, gmlp_h) = refs[7:10]
    (
        xs, hd, gains, wkv, wqo, wup, wdn,
        rx, sx, fl, gp, hidden, dkvf, dqf, mxf,
        snd, rr, ag, kvb, dks, dkr, pre, qd, scores, pd,
        gmlp, gatt, ra_m, rz_m, rb_m, rw_m, ra_a, rz_a, rb_a, rw_a, om, oa,
        load_sem, out_sem, send_sem, recv_sem,
    ) = refs[10:]
    sec = lax.axis_index("section")
    seq = lax.axis_index("seq")
    tp = lax.axis_index("tp")
    x_hi, z = seq // N_Z, lax.rem(seq, N_Z)
    quarter = rows // N_TP
    chunk = width // N_SEQ
    half = width // 2
    mine = pl.ds(pl.multiple_of(tp * quarter, quarter), quarter)

    def tp_dev(d):
        return {"tp": lax.rem(tp + d, N_TP)}

    def seq_dev(d):
        return {"seq": lax.rem(x_hi + d // N_Z, 2) * N_Z + lax.rem(z + d % N_Z, N_Z)}

    def seq_back(d):
        return {"seq": lax.rem(x_hi + d // N_Z, 2) * N_Z + lax.rem(z + N_Z - d % N_Z, N_Z)}

    def sec_dev(by, d):
        return {"section": lax.rem(sec + by, N_SEC), "tp": lax.rem(tp + d, N_TP)}

    barrier = pltpu.get_barrier_semaphore()
    for d in range(1, N_TP):
        pl.semaphore_signal(barrier, inc=1, device_id=tp_dev(d), device_id_type=MESH)
    for d in range(1, N_SEQ):
        pl.semaphore_signal(barrier, inc=1, device_id=seq_dev(d), device_id_type=MESH)
    for d in range(N_TP):
        pl.semaphore_signal(barrier, inc=1, device_id=sec_dev(1, d), device_id_type=MESH)

    loads = []
    for k, (src, dst) in enumerate(
        ((streams_h, xs), (gains_h, gains), (wup_h, wup), (wdn_h, wdn), (wkv_h, wkv), (wqo_h, wqo), (head_h, hd))
    ):
        copy = pltpu.make_async_copy(src, dst, load_sem.at[k])
        copy.start()
        loads.append(copy)
    sender = Sender(send_sem, recv_sem)

    lane = lax.broadcasted_iota(jnp.int32, (rows, PAIR), 1)
    lane_all = lax.rem(lax.broadcasted_iota(jnp.int32, (rows, att), 1), PAIR)

    def peer_rows(d):
        return pl.ds(pl.multiple_of(lax.rem(tp + d, N_TP) * quarter, quarter), quarter)

    def scatter(t, k):
        return [
            sender.start(snd.at[t, k, peer_rows(d), :], rr.at[t, k, d - 1], tp_dev(d))
            for d in range(1, N_TP)
        ]

    def summed(t, k, copies):
        received(copies)
        total = snd[t, k, mine, :].astype(F32)
        for d in range(N_TP - 1):
            total = total + rr[t, k, d].astype(F32)
        return total

    def spread(slot, value):
        ag[slot, mine, :] = value.astype(BF16)
        return [
            sender.start(ag.at[slot, mine, :], ag.at[slot, mine, :], tp_dev(d)) for d in range(1, N_TP)
        ]

    def send_section(slot, value):
        sx[slot] = value.astype(BF16)
        return [
            sender.start(sx.at[slot], rx.at[slot * 3, mine, :], sec_dev(N_SEC - 1, d))
            for d in range(N_TP)
        ]

    def mlp_forward(t, x):
        gain = gains[1:2, :]

        def norm(r):
            unit, _ = unit_of(x[0, pl.ds(r, 32), :])
            fl[NU, pl.ds(t * rows + r, 32), :] = (unit * gain).astype(BF16)

        loop(rows // 32, 32, norm)

    def mlp_hidden(t):
        def up(c):
            out = dot(fl[NU, pl.ds(t * rows, rows), :], wup[:, pl.ds(c, 256)], NN)
            pre[:, pl.ds(c, 256)] = out
            hidden[pl.ds(t * rows, rows), pl.ds(c, 256)] = gelu(out).astype(BF16)

        loop(hid // 256, 256, up)

    def mlp_down(t):
        def down(c):
            snd[t, 0, :, pl.ds(c, 256)] = dot(
                hidden[pl.ds(t * rows, rows), :], wdn[pl.ds(c, 256), :], NT
            ).astype(BF16)

        loop(width // 256, 256, down)

    def mlp_back(t, x):
        def low(r):
            fl[GL, pl.ds(t * rows + r, 32), :] = x[3, pl.ds(r, 32), :].astype(BF16)

        loop(rows // 32, 32, low)

        def back(c):
            grad = dot(fl[GL, pl.ds(t * rows, rows), :], wdn[:, pl.ds(c, 256)], NN)
            gp[pl.ds(t * rows, rows), pl.ds(c, 256)] = (
                grad * gelu_slope(pre[:, pl.ds(c, 256)])
            ).astype(BF16)

        loop(hid // 256, 256, back)

        def out(c):
            snd[t, 1, :, pl.ds(c, 256)] = dot(
                gp[pl.ds(t * rows, rows), :], wup[pl.ds(c, 256), :], NT
            ).astype(BF16)

        loop(width // 256, 256, out)
        return scatter(t, 1)

    def attention_in(t, x, slot):
        gain = gains[0:1, :]

        def low(r):
            value = x[1, pl.ds(r, 32), :] - ag[slot, pl.ds(r, 32), :].astype(F32)
            x[1, pl.ds(r, 32), :] = value
            if t == 0:
                rx_low[pl.ds(r, 32), :] = value.astype(BF16)
            unit, _ = unit_of(value)
            fl[AL, pl.ds(t * rows + r, 32), :] = (unit * gain).astype(BF16)

        rx_low = snd.at[0, 0]
        loop(rows // 32, 32, low)
        kvb[t, 0] = dot(fl[AL, pl.ds(t * rows, rows), :], wkv[...], NN).astype(BF16)
        copies = [
            sender.start(kvb.at[t, 0], kvb.at[t, d], seq_dev(d)) for d in range(1, N_SEQ)
        ]
        query = dot(fl[AL, pl.ds(t * rows, rows), :], wqo[...], NN).astype(BF16).astype(F32) * 0.125
        qd[pl.ds(0, rows), :] = jnp.where(lane_all < HEAD_DIM, query, 0.0).astype(BF16)
        return copies

    def grads_in(t, x, slot):
        gain = gains[1:2, :]

        def total(r):
            grad = ag[slot, pl.ds(r, 32), :].astype(F32)
            value = x[2, pl.ds(r, 32), :] + norm_back(grad, gain, x[0, pl.ds(r, 32), :])
            x[2, pl.ds(r, 32), :] = value
            fl[TL, pl.ds(t * rows + r, 32), :] = value.astype(BF16)

        loop(rows // 32, 32, total)
        grad = dot(fl[TL, pl.ds(t * rows, rows), :], wqo[...], NN)
        qd[pl.ds(rows, rows), :] = jnp.where(lane_all >= HEAD_DIM, grad, 0.0).astype(BF16)

    def attend(t):
        tokens = N_SEQ * rows

        def head(c):
            lanes = pl.ds(c, PAIR)
            kv = kvb[t, :, :, lanes].reshape(tokens, PAIR)
            both = qd[:, lanes]
            scores[...] = dot(kv, both, NT)
            logits = scores[:, :rows]
            weight = jnp.exp(logits - jnp.max(logits, 0, keepdims=True))
            probs = weight * (1.0 / jnp.sum(weight, 0, keepdims=True))
            grad_probs = scores[:, rows:]
            delta = jnp.sum(probs * grad_probs, 0, keepdims=True)
            pd[:, rows:] = probs.astype(BF16)
            pd[:, :rows] = (probs * (grad_probs - delta)).astype(BF16)
            dks[t, :, :, lanes] = dot(pd[...], both, NN).astype(BF16).reshape(N_SEQ, rows, PAIR)
            mixed = dot(pd[...], kv, TN)
            dqf[pl.ds(t * rows, rows), lanes] = jnp.where(lane < HEAD_DIM, mixed[:rows] * 0.125, 0.0).astype(BF16)
            mxf[pl.ds(t * rows, rows), lanes] = jnp.where(lane >= HEAD_DIM, mixed[rows:], 0.0).astype(BF16)

        loop(att // PAIR, PAIR, head)
        return [
            sender.start(dks.at[t, d], dkr.at[t, d - 1], seq_back(d)) for d in range(1, N_SEQ)
        ]

    def attention_out(t):
        def out(c):
            snd[t, 2, :, pl.ds(c, 256)] = dot(
                mxf[pl.ds(t * rows, rows), :], wqo[pl.ds(c, 256), :], NT
            ).astype(BF16)

        loop(width // 256, 256, out)
        return scatter(t, 2)

    def attention_back(t, copies):
        received(copies)

        def add(r):
            total = dks[t, 0, pl.ds(r, 32), :].astype(F32)
            for d in range(N_SEQ - 1):
                total = total + dkr[t, d, pl.ds(r, 32), :].astype(F32)
            dkvf[pl.ds(t * rows + r, 32), :] = total.astype(BF16)

        loop(rows // 32, 32, add)

        def out(c):
            snd[t, 3, :, pl.ds(c, 256)] = (
                dot(dkvf[pl.ds(t * rows, rows), :], wkv[pl.ds(c, 256), :], NT)
                + dot(dqf[pl.ds(t * rows, rows), :], wqo[pl.ds(c, 256), :], NT)
            ).astype(BF16)

        loop(width // 256, 256, out)
        return scatter(t, 3)

    def grad_rows(by_x, by_z):
        index = lax.rem(x_hi + by_x, 2) * N_Z + lax.rem(z + by_z, N_Z)
        return pl.ds(pl.multiple_of(index * chunk, 32), chunk)

    def reduce_first(g, cut, ra, rb):
        other = pl.ds(pl.multiple_of((1 - x_hi) * half, 32), half)
        cols_a, cols_b = pl.ds(0, cut), pl.ds(cut, g.shape[1] - cut)
        first = [sender.start(g.at[other, cols_a], ra, seq_dev(N_Z))]
        second = []
        for d in range(1, N_Z):
            for k in range(2):
                second.append(sender.start(g.at[grad_rows(k, d), cols_b], rb.at[d - 1, k], seq_dev(d)))
        return first, second

    def reduce_second(g, cut, ra, rb, rz, rw, copies):
        first, second = copies
        cols_a, cols_b = pl.ds(0, cut), pl.ds(cut, g.shape[1] - cut)
        base = x_hi * half
        received(first)

        def add_a(r):
            here = pl.ds(pl.multiple_of(base + r, 32), 32)
            g[here, cols_a] = (g[here, cols_a].astype(F32) + ra[pl.ds(r, 32), :].astype(F32)).astype(BF16)

        loop(half // 32, 32, add_a)
        out = [
            sender.start(g.at[grad_rows(0, d), cols_a], rz.at[d - 1], seq_dev(d)) for d in range(1, N_Z)
        ]
        received(second)
        for k in (1, 0):
            start = (lax.rem(x_hi + k, 2) * N_Z + z) * chunk

            def add_b(r):
                here = pl.ds(pl.multiple_of(start + r, 32), 32)
                total = g[here, cols_b].astype(F32)
                for d in range(N_Z - 1):
                    total = total + rb[d, k, pl.ds(r, 32), :].astype(F32)
                g[here, cols_b] = total.astype(BF16)

            loop(chunk // 32, 32, add_b)
            if k == 1:
                out.append(sender.start(g.at[grad_rows(1, 0), cols_b], rw, seq_dev(N_Z)))
        return out

    def reduce_last(g, cut, rz, rw, out, dst, copies, sem):
        cols_a, cols_b = pl.ds(0, cut), pl.ds(cut, g.shape[1] - cut)
        received(copies)
        start = seq * chunk

        def add(r):
            here = pl.ds(pl.multiple_of(start + r, 32), 32)
            total = g[here, cols_a].astype(F32)
            for d in range(N_Z - 1):
                total = total + rz[d, pl.ds(r, 32), :].astype(F32)
            out[pl.ds(r, 32), cols_a] = total.astype(BF16)
            out[pl.ds(r, 32), cols_b] = (
                g[here, cols_b].astype(F32) + rw[pl.ds(r, 32), :].astype(F32)
            ).astype(BF16)

        loop(chunk // 32, 32, add)
        copy = pltpu.make_async_copy(out, dst, sem)
        copy.start()
        return copy

    def grads_mlp():
        def tile(c):
            gmlp[pl.ds(c, 256), pl.ds(0, hid)] = dot(fl[NU, :, pl.ds(c, 256)], gp[...], TN).astype(BF16)
            gmlp[pl.ds(c, 256), pl.ds(hid, hid)] = dot(fl[GL, :, pl.ds(c, 256)], hidden[...], TN).astype(BF16)

        loop(width // 256, 256, tile)
        return reduce_first(gmlp, cut_mlp, ra_m, rb_m)

    def grads_att():
        def tile(c):
            left = fl[AL, :, pl.ds(c, 256)]
            gatt[pl.ds(c, 256), pl.ds(0, att)] = dot(left, dkvf[...], TN).astype(BF16)
            gatt[pl.ds(c, 256), pl.ds(att, att)] = (
                dot(left, dqf[...], TN) + dot(fl[TL, :, pl.ds(c, 256)], mxf[...], TN)
            ).astype(BF16)

        loop(width // 256, 256, tile)
        return reduce_first(gatt, cut_att, ra_a, rb_a)

    loads[0].wait()
    loads[1].wait()
    mlp_forward(0, xs)
    loads[2].wait()
    mlp_hidden(0)
    loads[3].wait()
    mlp_down(0)
    pl.semaphore_wait(barrier, N_TP - 1 + N_SEQ - 1 + N_TP)
    c_mlp = scatter(0, 0)
    c_grad = mlp_back(0, xs)
    c_mlp = spread(0, summed(0, 0, c_mlp))
    c_grad = spread(1, summed(0, 1, c_grad))
    received(c_mlp)
    loads[4].wait()
    loads[5].wait()
    for copy in sender.all[:3]:
        copy.wait_send()
    c_kv = attention_in(0, xs, 0)
    c_low = sender.start(snd.at[0, 0], rx.at[1], sec_dev(N_SEC - 1, 0))
    received(c_grad)
    grads_in(0, xs, 1)
    c_total = sender.start(fl.at[TL, pl.ds(0, rows), :], rx.at[2], sec_dev(N_SEC - 1, 0))
    received(c_kv)
    c_dkv = attend(0)
    c_att = attention_out(0)
    c_up = send_section(0, xs[0, mine, :] - summed(0, 2, c_att))

    is_last = sec == N_SEC - 1
    loads[6].wait()

    def choose(k):
        def one(r):
            hd[k, pl.ds(r, 32), :] = jnp.where(
                is_last, hd[k, pl.ds(r, 32), :], rx[k, pl.ds(r, 32), :].astype(F32)
            )

        loop(rows // 32, 32, one)

    outs = []

    def emit(k):
        copy = pltpu.make_async_copy(hd.at[k], recon_h.at[k], out_sem.at[k])
        copy.start()
        outs.append(copy)

    slope = gains[0:1, :]
    c_att = attention_back(0, c_dkv)
    received(c_up)
    choose(0)
    mlp_forward(1, hd)
    mlp_hidden(1)
    mlp_down(1)
    c_mlp = scatter(1, 0)
    grad = summed(0, 3, c_att)
    c_gl = send_section(1, xs[3, mine, :] + norm_back(grad, slope, xs[1, mine, :]))
    c_mlp = spread(2, summed(1, 0, c_mlp))
    received([c_low])
    choose(1)
    received(c_mlp)
    c_kv = attention_in(1, hd, 2)
    emit(1)
    received(c_gl)
    choose(3)
    c_grad = mlp_back(1, hd)
    c_gm = grads_mlp()
    c_grad = spread(3, summed(1, 1, c_grad))
    received([c_total])
    choose(2)
    received(c_grad)
    grads_in(1, hd, 3)
    emit(2)
    received(c_kv)
    c_dkv = attend(1)
    c_att = attention_out(1)
    c_up = spread(4, summed(1, 2, c_att))
    c_att = attention_back(1, c_dkv)
    c_ga = grads_att()
    c_gl = spread(5, summed(1, 3, c_att))
    c_gm = reduce_second(gmlp, cut_mlp, ra_m, rb_m, rz_m, rw_m, c_gm)
    received(c_up)

    def upper(r):
        here = pl.ds(r, 32)
        value = hd[0, here, :]
        pre[here, :] = value - ag[4, here, :].astype(F32)

    loop(rows // 32, 32, upper)
    copy = pltpu.make_async_copy(pre, recon_h.at[0], out_sem.at[0])
    copy.start()
    outs.append(copy)
    received(c_gl)

    def lower(r):
        here = pl.ds(r, 32)
        hd[3, here, :] = hd[3, here, :] + norm_back(
            ag[5, here, :].astype(F32), slope, xs_low(here)
        )

    def xs_low(here):
        return hd[1, here, :]

    loop(rows // 32, 32, lower)
    emit(3)
    c_ga = reduce_second(gatt, cut_att, ra_a, rb_a, rz_a, rw_a, c_ga)
    outs.append(reduce_last(gmlp, cut_mlp, rz_m, rw_m, om, gmlp_h, c_gm, out_sem.at[4]))
    outs.append(reduce_last(gatt, cut_att, rz_a, rw_a, oa, gatt_h, c_ga, out_sem.at[5]))
    for copy in sender.all[3:]:
        copy.wait_send()
    for copy in outs:
        copy.wait()


N_COPIES = 104


def per_device(streams, head_streams, gains, w_qkv, w_out, w_up, w_down):
    rows, width = streams.shape[2], streams.shape[3]
    hid = w_up.shape[2]
    local = w_out.shape[2]
    att = 2 * local
    heads = local // HEAD_DIM
    chunk = width // N_SEQ
    half = width // 2
    cut_mlp = 1536
    cut_att = 768
    parts = w_qkv[0].reshape(width, 3, heads, HEAD_DIM)
    w_o = w_out[0].reshape(width, heads, HEAD_DIM)
    wkv = jnp.stack([parts[:, 1], parts[:, 2]], 2).reshape(width, att)
    wqo = jnp.stack([parts[:, 0], w_o], 2).reshape(width, att)
    sizes = (rows, width, hid, att, cut_mlp, cut_att)
    quarter = rows // N_TP
    rest_m, rest_a = 2 * hid - cut_mlp, 2 * att - cut_att
    vm = pltpu.VMEM
    scratch = [
        vm((4, rows, width), F32), vm((4, rows, width), F32), vm((2, width), F32),
        vm((width, att), BF16), vm((width, att), BF16), vm((width, hid), BF16), vm((width, hid), BF16),
        vm((4, rows, width), BF16), vm((2, quarter, width), BF16),
        vm((4, 2 * rows, width), BF16), vm((2 * rows, hid), BF16), vm((2 * rows, hid), BF16),
        vm((2 * rows, att), BF16), vm((2 * rows, att), BF16), vm((2 * rows, att), BF16),
        vm((2, 4, rows, width), BF16), vm((2, 4, N_TP - 1, quarter, width), BF16), vm((6, rows, width), BF16),
        vm((2, N_SEQ, rows, att), BF16), vm((2, N_SEQ, rows, att), BF16), vm((2, N_SEQ - 1, rows, att), BF16),
        vm((rows, hid), F32), vm((2 * rows, att), BF16),
        vm((N_SEQ * rows, 2 * rows), F32), vm((N_SEQ * rows, 2 * rows), BF16),
        vm((width, 2 * hid), BF16), vm((width, 2 * att), BF16),
        vm((half, cut_mlp), BF16), vm((N_Z - 1, chunk, cut_mlp), BF16),
        vm((N_Z - 1, 2, chunk, rest_m), BF16), vm((chunk, rest_m), BF16),
        vm((half, cut_att), BF16), vm((N_Z - 1, chunk, cut_att), BF16),
        vm((N_Z - 1, 2, chunk, rest_a), BF16), vm((chunk, rest_a), BF16),
        vm((chunk, 2 * hid), BF16), vm((chunk, 2 * att), BF16),
        pltpu.SemaphoreType.DMA((7,)), pltpu.SemaphoreType.DMA((6,)),
        pltpu.SemaphoreType.DMA((N_COPIES,)), pltpu.SemaphoreType.DMA((N_COPIES,)),
    ]
    any_spec = pl.BlockSpec(memory_space=pl.ANY)
    recon, gatt, gmlp = pl.pallas_call(
        lambda *refs: kernel(sizes, *refs),
        out_shape=(
            jax.ShapeDtypeStruct((4, rows, width), F32),
            jax.ShapeDtypeStruct((chunk, 2 * att), BF16),
            jax.ShapeDtypeStruct((chunk, 2 * hid), BF16),
        ),
        in_specs=[any_spec] * 7,
        out_specs=(any_spec,) * 3,
        scratch_shapes=scratch,
        compiler_params=pltpu.CompilerParams(
            collective_id=0, has_side_effects=True, vmem_limit_bytes=67043328
        ),
        name="window",
    )(streams[0], head_streams, gains[0], wkv, wqo, w_up[0], w_down[0])
    pairs = gatt.reshape(chunk, 2, heads, 2, HEAD_DIM)
    grad_qkv = jnp.stack([pairs[:, 1, :, 0], pairs[:, 0, :, 0], pairs[:, 0, :, 1]], 1).reshape(chunk, 3, local)
    grad_out = pairs[:, 1, :, 1].reshape(chunk, local)
    return (recon[None], grad_qkv[None], grad_out[None], gmlp[None, :, :hid], gmlp[None, :, hid:])


def solution(mesh):
    return jax.shard_map(
        per_device,
        mesh=mesh,
        in_specs=(
            P("section", None, "seq", None),
            P(None, "seq", None),
            P("section", None, None),
            P("section", None, None, "tp"),
            P("section", None, "tp"),
            P("section", None, "tp"),
            P("section", None, "tp"),
        ),
        out_specs=(
            P("section", None, "seq", None),
            P("section", "seq", None, "tp"),
            P("section", "seq", "tp"),
            P("section", "seq", "tp"),
            P("section", "seq", "tp"),
        ),
        check_vma=False,
    )
```

time: 588 us -> 230 us (0.39); the launches traced: 577 us -> 229 us
  waiting for transfers between devices: 328 us -> 0 us
  Pallas kernels: 0 us -> 213 us
  starting transfers between devices: 69.1 us -> 0 us
  matrix products: 58.8 us -> 0 us
  other arithmetic: 53.5 us -> 1.46 us
  local copies, waits for them, and re-layouts: 52.9 us -> 13.5 us
  between operations: 15.5 us -> 0.68 us
    pallas_call x0 -> x1, Pallas kernels: none -> 213 us  [per_device(): pl.pallas_call(lambda *refs: kernel(sizes, *refs), out_shape=(jax.ShapeDt...]
    reduce_scatter x8 -> x0, waiting for transfers between devices: 184 us -> none  [own_block(): tiles = lax.psum_scatter(tiles, axes[k], scatter_dimension=0, tiled=True)]
    all_to_all x12 -> x0, waiting for transfers between devices: 128 us -> none  [the longest x10 109 us: copy_for_each(): return lax.all_to_all(copies, axis, split_axis=0, concat_axis=0, tiled=True)]
    all_to_all x12 -> x0, starting transfers between devices: 63.1 us -> none  [the longest x10 51.2 us: copy_for_each(): return lax.all_to_all(copies, axis, split_axis=0, concat_axis=0, tiled=True)]
    dot_general x36 -> x0, matrix products: 58.8 us -> none  [the longest x2 8.89 us: block_step(): jnp.dot(att_low.T, grad_proj, preferred_element_type=jnp.float32)]
    reduce_sum x22 -> x0, other arithmetic: 35.2 us -> none  [the longest x6 13.2 us: taken_together(): return jnp.sum(everything.astype(jnp.float32), axis=0)]
    broadcast_in_dim x10 -> x1, local copies, waits for them, and re-layouts: 18 us -> 2.06 us  [per_device(): gmlp[None, :, hid:]]
    ppermute x1 -> x0, waiting for transfers between devices: 15.8 us -> none  [from_behind(): return lax.ppermute(shard, axis, pairs)]
  transfers between devices with their start and end apart: 21 -> 0, of which waited for: 19 -> 0; matrix products, arithmetic and copies ran while one was open for 13% -> 0% of each run, Pallas kernels for 0% -> 0%
where the time goes in v1:
time: 230 us; the launch traced here: 229 us
  Pallas kernels  213 us (93%)
  local copies, waits for them, and re-layouts  13.5 us (6%)
    pallas_call x1, Pallas kernels, per_device(): pl.pallas_call(lambda *refs: kernel(sizes, *refs), out_shape=(jax.ShapeDt...  213 us

profile of v1, /device:TPU:1, one launch (start us, length us, event | category | flops | bytes accessed | tf_op | source)
XLA Modules:
  0.0 228.6 jit_solution(9654040385317936844)
XLA Ops:
  0.6 0.0 copy-start.1
  0.6 1.9 slice_bitcast_fusion
  2.5 0.0 copy-done.1
  2.5 0.3 pad_maximum_fusion
  2.8 2.2 copy.16.refs_3_
  5.0 2.2 copy.17.refs_4_
  7.2 213.0 %window.1 = (f32[4,128,1280]{2,1,0:T(8,128)}, bf16[160,1280]{1,0:T(8,128)(2,1)}, bf16[160,2560]{1,0:T(8,128)(2,1)}) custom-call(f32[4,128,1280]{2,1,0:T(8,128)} %bitcast.28, f32[4,128,1280]{2,1,0:T(8,128)} %refs_1_.1, f32[2,1280]{1,0:T(2,128)} %bitcast.37, bf16[1280,640]{1,0:T(8,128)(2,1)} %copy.16.refs_3_, bf16[1280,640]{1,0:T(8,128)(2,1)} %copy.17.refs_4_, ...), custom_call_target="tpu_custom_call" | custom-call | tf_op jit(solution)/shard_map/window/pallas_call | solution.py:542
  220.2 1.2 copy.18
  221.5 0.7 fusion
  222.2 0.8 copy.20
  222.9 0.0 copy-start
  222.9 1.2 pad_maximum_fusion.2
  224.1 1.0 copy.19
  225.1 2.1 slice_bitcast_fusion.3
  227.1 0.0 copy-done
  227.1 1.5 copy.22
Async XLA Ops:
  0.6 1.9 copy-start.1
  222.9 4.2 %copy-start = (f32[4,128,1280]{2,1,0:T(8,128)S(1)}, f32[4,128,1280]{2,1,0:T(8,128)}, u32[]{:S(2)}) copy-start(f32[4,128,1280]{2,1,0:T(8,128)} %get-tuple-element.8) | copy-start | bytes 7864324

commit v2 on v1

--- a/solution.py
+++ b/solution.py
@@ -16,6 +16,8 @@
 N_Z = 4
 N_SEQ = 8
 N_SEC = 4
+KV_X_FIRST = 2
+DKV_X_FIRST = 3
 NU, GL, AL, TL = 0, 1, 2, 3
 NN = (((1,), (0,)), ((), ()))
 NT = (((1,), (1,)), ((), ()))
@@ -89,15 +91,16 @@
 
 def kernel(sizes, *refs):
     rows, width, hid, att, cut_mlp, cut_att = sizes
-    (streams_h, head_h, gains_h, wkv_h, wqo_h, wup_h, wdn_h) = refs[:7]
-    (recon_h, gatt_h, gmlp_h) = refs[7:10]
+    (streams_h, head_h, gains_h, wqkv_h, wout_h, wup_h, wdn_h) = refs[:7]
+    (recon_h, gqkv_h, gout_h, gup_h, gdn_h) = refs[7:12]
     (
         xs, hd, gains, wkv, wqo, wup, wdn,
         rx, sx, fl, gp, hidden, dkvf, dqf, mxf,
-        snd, rr, ag, kvb, dks, dkr, pre, qd, scores, pd,
-        gmlp, gatt, ra_m, rz_m, rb_m, rw_m, ra_a, rz_a, rb_a, rw_a, om, oa,
+        snd, rr, ag, kvb, dks, dax, daz, dbz, dbx, pre, qd, scores, pd,
+        gmlp, gatt, ra_m, rz_m, rb_m, rw_m, ra_a, rz_a, rb_a, rw_a, om, oqkv, oout,
         load_sem, out_sem, send_sem, recv_sem,
-    ) = refs[10:]
+    ) = refs[12:]
+    heads = att // PAIR
     sec = lax.axis_index("section")
     seq = lax.axis_index("seq")
     tp = lax.axis_index("tp")
@@ -129,7 +132,11 @@
 
     loads = []
     for k, (src, dst) in enumerate(
-        ((streams_h, xs), (gains_h, gains), (wup_h, wup), (wdn_h, wdn), (wkv_h, wkv), (wqo_h, wqo), (head_h, hd))
+        (
+            (streams_h, xs), (gains_h, gains), (wup_h, wup), (wdn_h, wdn),
+            (wqkv_h.at[1], wkv.at[:, 0]), (wqkv_h.at[2], wkv.at[:, 1]),
+            (wqkv_h.at[0], wqo.at[:, 0]), (wout_h, wqo.at[:, 1]), (head_h, hd),
+        )
     ):
         copy = pltpu.make_async_copy(src, dst, load_sem.at[k])
         copy.start()
@@ -213,7 +220,6 @@
             ).astype(BF16)
 
         loop(width // 256, 256, out)
-        return scatter(t, 1)
 
     def attention_in(t, x, slot):
         gain = gains[0:1, :]
@@ -228,13 +234,37 @@
 
         rx_low = snd.at[0, 0]
         loop(rows // 32, 32, low)
-        kvb[t, 0] = dot(fl[AL, pl.ds(t * rows, rows), :], wkv[...], NN).astype(BF16)
-        copies = [
-            sender.start(kvb.at[t, 0], kvb.at[t, d], seq_dev(d)) for d in range(1, N_SEQ)
-        ]
-        query = dot(fl[AL, pl.ds(t * rows, rows), :], wqo[...], NN).astype(BF16).astype(F32) * 0.125
+        packed = dot(fl[AL, pl.ds(t * rows, rows), :], wkv[...].reshape(att, width), NT).astype(BF16)
+        across, along = [], []
+        for h in range(heads):
+            kvb[t, h, 0, 0] = packed[:, h * PAIR : (h + 1) * PAIR]
+            across.append(sender.start(kvb.at[t, h, 0, 0], kvb.at[t, h, 1, 0], seq_dev(N_Z)))
+            along.append(
+                [sender.start(kvb.at[t, h, 0, 0], kvb.at[t, h, 0, d], seq_dev(d)) for d in range(1, N_Z)]
+            )
+        query = dot(fl[AL, pl.ds(t * rows, rows), :], wqo[...].reshape(att, width), NT)
+        query = query.astype(BF16).astype(F32) * 0.125
         qd[pl.ds(0, rows), :] = jnp.where(lane_all < HEAD_DIM, query, 0.0).astype(BF16)
-        return copies
+        return across, along
+
+    def pass_along(t, copies):
+        across, along = copies
+        late = []
+        for h in range(KV_X_FIRST):
+            received([across[h]])
+            late.append(
+                [sender.start(kvb.at[t, h, 1, 0], kvb.at[t, h, 1, d], seq_dev(d)) for d in range(1, N_Z)]
+            )
+        return late
+
+    def pass_across(t, copies, late):
+        across, along = copies
+        for h in range(KV_X_FIRST, heads):
+            received(along[h])
+            late.append(
+                [sender.start(kvb.at[t, h, 0, d], kvb.at[t, h, 1, d], seq_dev(N_Z)) for d in range(1, N_Z)]
+            )
+        return late
 
     def grads_in(t, x, slot):
         gain = gains[1:2, :]
@@ -246,15 +276,21 @@
             fl[TL, pl.ds(t * rows + r, 32), :] = value.astype(BF16)
 
         loop(rows // 32, 32, total)
-        grad = dot(fl[TL, pl.ds(t * rows, rows), :], wqo[...], NN)
+        grad = dot(fl[TL, pl.ds(t * rows, rows), :], wqo[...].reshape(att, width), NT)
         qd[pl.ds(rows, rows), :] = jnp.where(lane_all >= HEAD_DIM, grad, 0.0).astype(BF16)
 
-    def attend(t):
+    def attend(t, copies, late):
+        across, along = copies
         tokens = N_SEQ * rows
-
-        def head(c):
-            lanes = pl.ds(c, PAIR)
-            kv = kvb[t, :, :, lanes].reshape(tokens, PAIR)
+        first = []
+        for h in range(heads):
+            lanes = pl.ds(h * PAIR, PAIR)
+            if h < KV_X_FIRST:
+                received(along[h])
+            else:
+                received([across[h]])
+            received(late[h])
+            kv = kvb[t, h].reshape(tokens, PAIR)
             both = qd[:, lanes]
             scores[...] = dot(kv, both, NT)
             logits = scores[:, :rows]
@@ -264,40 +300,67 @@
             delta = jnp.sum(probs * grad_probs, 0, keepdims=True)
             pd[:, rows:] = probs.astype(BF16)
             pd[:, :rows] = (probs * (grad_probs - delta)).astype(BF16)
-            dks[t, :, :, lanes] = dot(pd[...], both, NN).astype(BF16).reshape(N_SEQ, rows, PAIR)
+            dks[t, h] = dot(pd[...], both, NN).astype(BF16).reshape(2, N_Z, rows, PAIR)
+            if h < DKV_X_FIRST:
+                first.append([sender.start(dks.at[t, h, 1], dax.at[t, h], seq_dev(N_Z))])
+            else:
+                first.append(
+                    [
+                        sender.start(dks.at[t, h, :, d], dbz.at[t, h - DKV_X_FIRST, d - 1], seq_back(d))
+                        for d in range(1, N_Z)
+                    ]
+                )
             mixed = dot(pd[...], kv, TN)
             dqf[pl.ds(t * rows, rows), lanes] = jnp.where(lane < HEAD_DIM, mixed[:rows] * 0.125, 0.0).astype(BF16)
             mxf[pl.ds(t * rows, rows), lanes] = jnp.where(lane >= HEAD_DIM, mixed[rows:], 0.0).astype(BF16)
-
-        loop(att // PAIR, PAIR, head)
-        return [
-            sender.start(dks.at[t, d], dkr.at[t, d - 1], seq_back(d)) for d in range(1, N_SEQ)
-        ]
+        return first
 
     def attention_out(t):
         def out(c):
             snd[t, 2, :, pl.ds(c, 256)] = dot(
-                mxf[pl.ds(t * rows, rows), :], wqo[pl.ds(c, 256), :], NT
+                mxf[pl.ds(t * rows, rows), :], wqo[:, :, :, pl.ds(c, 256)].reshape(att, 256), NN
             ).astype(BF16)
 
         loop(width // 256, 256, out)
         return scatter(t, 2)
 
-    def attention_back(t, copies):
-        received(copies)
-
-        def add(r):
-            total = dks[t, 0, pl.ds(r, 32), :].astype(F32)
-            for d in range(N_SEQ - 1):
-                total = total + dkr[t, d, pl.ds(r, 32), :].astype(F32)
-            dkvf[pl.ds(t * rows + r, 32), :] = total.astype(BF16)
-
-        loop(rows // 32, 32, add)
+    def attention_relay(t, first):
+        last = []
+        for h in range(heads):
+            received(first[h])
+            if h < DKV_X_FIRST:
+                for d in (1, 2, 3, 0):
+                    dks[t, h, 0, d] = (
+                        dks[t, h, 0, d].astype(F32) + dax[t, h, d].astype(F32)
+                    ).astype(BF16)
+                    if d > 0:
+                        last.append(sender.start(dks.at[t, h, 0, d], daz.at[t, h, d - 1], seq_back(d)))
+            else:
+                k = h - DKV_X_FIRST
+                for side in (1, 0):
+                    total = dks[t, h, side, 0].astype(F32)
+                    for d in range(N_Z - 1):
+                        total = total + dbz[t, k, d, side].astype(F32)
+                    dks[t, h, side, 0] = total.astype(BF16)
+                last.append(sender.start(dks.at[t, h, 1, 0], dbx.at[t, k], seq_dev(N_Z)))
+        return last
+
+    def attention_back(t, last):
+        received(last)
+        for h in range(heads):
+            total = dks[t, h, 0, 0].astype(F32)
+            if h < DKV_X_FIRST:
+                for d in range(N_Z - 1):
+                    total = total + daz[t, h, d].astype(F32)
+            else:
+                total = total + dbx[t, h - DKV_X_FIRST].astype(F32)
+            dkvf[pl.ds(t * rows, rows), pl.ds(h * PAIR, PAIR)] = total.astype(BF16)
 
         def out(c):
-            snd[t, 3, :, pl.ds(c, 256)] = (
-                dot(dkvf[pl.ds(t * rows, rows), :], wkv[pl.ds(c, 256), :], NT)
-                + dot(dqf[pl.ds(t * rows, rows), :], wqo[pl.ds(c, 256), :], NT)
+            cols = pl.ds(c, 256)
+            snd[t, 3, :, cols] = (
+                dot(dkvf[pl.ds(t * rows, rows), :], wkv[:, :, :, cols].reshape(att, 256), NN)
+                + dot(dqf[pl.ds(t * rows, rows), :], wqo[:, :, :, cols].reshape(att, 256), NN)
             ).astype(BF16)
 
         loop(width // 256, 256, out)
@@ -347,7 +410,7 @@
                 out.append(sender.start(g.at[grad_rows(1, 0), cols_b], rw, seq_dev(N_Z)))
         return out
 
-    def reduce_last(g, cut, rz, rw, out, dst, copies, sem):
+    def reduce_last(g, cut, rz, rw, store, copies):
         cols_a, cols_b = pl.ds(0, cut), pl.ds(cut, g.shape[1] - cut)
         received(copies)
         start = seq * chunk
@@ -357,15 +420,30 @@
             total = g[here, cols_a].astype(F32)
             for d in range(N_Z - 1):
                 total = total + rz[d, pl.ds(r, 32), :].astype(F32)
-            out[pl.ds(r, 32), cols_a] = total.astype(BF16)
-            out[pl.ds(r, 32), cols_b] = (
-                g[here, cols_b].astype(F32) + rw[pl.ds(r, 32), :].astype(F32)
-            ).astype(BF16)
+            rest = g[here, cols_b].astype(F32) + rw[pl.ds(r, 32), :].astype(F32)
+            store(pl.ds(r, 32), total.astype(BF16), rest.astype(BF16))
 
         loop(chunk // 32, 32, add)
-        copy = pltpu.make_async_copy(out, dst, sem)
-        copy.start()
-        return copy
+
+    def store_mlp(here, left, right):
+        om[0, here, :] = left[:, :hid]
+        om[1, here, pl.ds(0, cut_mlp - hid)] = left[:, hid:]
+        om[1, here, pl.ds(cut_mlp - hid, 2 * hid - cut_mlp)] = right
+
+    def store_att(here, left, right):
+        def piece(p, h, k):
+            start = p * att + h * PAIR + k * HEAD_DIM
+            if start < cut_att:
+                return left[:, start : start + HEAD_DIM]
+            return right[:, start - cut_att : start - cut_att + HEAD_DIM]
+
+        def joined(p, k):
+            return jnp.concatenate([piece(p, h, k) for h in range(heads)], 1)
+
+        oqkv[0, here, :] = joined(1, 0)
+        oqkv[1, here, :] = joined(0, 0)
+        oqkv[2, here, :] = joined(0, 1)
+        oout[here, :] = joined(1, 1)
 
     def grads_mlp():
         def tile(c):
@@ -395,26 +473,29 @@
     mlp_down(0)
     pl.semaphore_wait(barrier, N_TP - 1 + N_SEQ - 1 + N_TP)
     c_mlp = scatter(0, 0)
-    c_grad = mlp_back(0, xs)
+    mlp_back(0, xs)
     c_mlp = spread(0, summed(0, 0, c_mlp))
-    c_grad = spread(1, summed(0, 1, c_grad))
     received(c_mlp)
-    loads[4].wait()
-    loads[5].wait()
+    c_grad = scatter(0, 1)
+    for k in range(4, 8):
+        loads[k].wait()
     for copy in sender.all[:3]:
         copy.wait_send()
     c_kv = attention_in(0, xs, 0)
-    c_low = sender.start(snd.at[0, 0], rx.at[1], sec_dev(N_SEC - 1, 0))
+    late = pass_along(0, c_kv)
+    c_grad = spread(1, summed(0, 1, c_grad))
+    late = pass_across(0, c_kv, late)
     received(c_grad)
     grads_in(0, xs, 1)
+    c_dkv = attend(0, c_kv, late)
+    c_att = attention_out(0)
+    c_dkv = attention_relay(0, c_dkv)
+    c_up = send_section(0, xs[0, mine, :] - summed(0, 2, c_att))
+    c_low = sender.start(snd.at[0, 0], rx.at[1], sec_dev(N_SEC - 1, 0))
     c_total = sender.start(fl.at[TL, pl.ds(0, rows), :], rx.at[2], sec_dev(N_SEC - 1, 0))
-    received(c_kv)
-    c_dkv = attend(0)
-    c_att = attention_out(0)
-    c_up = send_section(0, xs[0, mine, :] - summed(0, 2, c_att))
 
     is_last = sec == N_SEC - 1
-    loads[6].wait()
+    loads[8].wait()
 
     def choose(k):
         def one(r):
@@ -428,6 +509,11 @@
 
     def emit(k):
         copy = pltpu.make_async_copy(hd.at[k], recon_h.at[k], out_sem.at[k])
+        copy.start()
+        outs.append(copy)
+
+    def finish(src, dst, k):
+        copy = pltpu.make_async_copy(src, dst, out_sem.at[k])
         copy.start()
         outs.append(copy)
 
@@ -449,7 +535,9 @@
     emit(1)
     received(c_gl)
     choose(3)
-    c_grad = mlp_back(1, hd)
+    late = pass_across(1, c_kv, pass_along(1, c_kv))
+    mlp_back(1, hd)
+    c_grad = scatter(1, 1)
     c_gm = grads_mlp()
     c_grad = spread(3, summed(1, 1, c_grad))
     received([c_total])
@@ -457,9 +545,9 @@
     received(c_grad)
     grads_in(1, hd, 3)
     emit(2)
-    received(c_kv)
-    c_dkv = attend(1)
+    c_dkv = attend(1, c_kv, late)
     c_att = attention_out(1)
+    c_dkv = attention_relay(1, c_dkv)
     c_up = spread(4, summed(1, 2, c_att))
     c_att = attention_back(1, c_dkv)
     c_ga = grads_att()
@@ -490,15 +578,19 @@
     loop(rows // 32, 32, lower)
     emit(3)
     c_ga = reduce_second(gatt, cut_att, ra_a, rb_a, rz_a, rw_a, c_ga)
-    outs.append(reduce_last(gmlp, cut_mlp, rz_m, rw_m, om, gmlp_h, c_gm, out_sem.at[4]))
-    outs.append(reduce_last(gatt, cut_att, rz_a, rw_a, oa, gatt_h, c_ga, out_sem.at[5]))
+    reduce_last(gmlp, cut_mlp, rz_m, rw_m, store_mlp, c_gm)
+    finish(om.at[0], gup_h, 4)
+    finish(om.at[1], gdn_h, 5)
+    reduce_last(gatt, cut_att, rz_a, rw_a, store_att, c_ga)
+    finish(oqkv, gqkv_h, 6)
+    finish(oout, gout_h, 7)
     for copy in sender.all[3:]:
         copy.wait_send()
     for copy in outs:
         copy.wait()
 
 
-N_COPIES = 104
+N_COPIES = 240
 
 
 def per_device(streams, head_streams, gains, w_qkv, w_out, w_up, w_down):
@@ -511,22 +603,24 @@
     half = width // 2
     cut_mlp = 1536
     cut_att = 768
-    parts = w_qkv[0].reshape(width, 3, heads, HEAD_DIM)
-    w_o = w_out[0].reshape(width, heads, HEAD_DIM)
-    wkv = jnp.stack([parts[:, 1], parts[:, 2]], 2).reshape(width, att)
-    wqo = jnp.stack([parts[:, 0], w_o], 2).reshape(width, att)
+    wqkv = jnp.transpose(w_qkv[0], (1, 2, 0)).reshape(3, heads, HEAD_DIM, width)
+    wout = jnp.transpose(w_out[0], (1, 0)).reshape(heads, HEAD_DIM, width)
     sizes = (rows, width, hid, att, cut_mlp, cut_att)
     quarter = rows // N_TP
     rest_m, rest_a = 2 * hid - cut_mlp, 2 * att - cut_att
+    n_dx, n_dz = DKV_X_FIRST, heads - DKV_X_FIRST
     vm = pltpu.VMEM
     scratch = [
         vm((4, rows, width), F32), vm((4, rows, width), F32), vm((2, width), F32),
-        vm((width, att), BF16), vm((width, att), BF16), vm((width, hid), BF16), vm((width, hid), BF16),
+        vm((heads, 2, HEAD_DIM, width), BF16), vm((heads, 2, HEAD_DIM, width), BF16),
+        vm((width, hid), BF16), vm((width, hid), BF16),
         vm((4, rows, width), BF16), vm((2, quarter, width), BF16),
         vm((4, 2 * rows, width), BF16), vm((2 * rows, hid), BF16), vm((2 * rows, hid), BF16),
         vm((2 * rows, att), BF16), vm((2 * rows, att), BF16), vm((2 * rows, att), BF16),
         vm((2, 4, rows, width), BF16), vm((2, 4, N_TP - 1, quarter, width), BF16), vm((6, rows, width), BF16),
-        vm((2, N_SEQ, rows, att), BF16), vm((2, N_SEQ, rows, att), BF16), vm((2, N_SEQ - 1, rows, att), BF16),
+        vm((2, heads, 2, N_Z, rows, PAIR), BF16), vm((2, heads, 2, N_Z, rows, PAIR), BF16),
+        vm((2, n_dx, N_Z, rows, PAIR), BF16), vm((2, n_dx, N_Z - 1, rows, PAIR), BF16),
+        vm((2, n_dz, N_Z - 1, 2, rows, PAIR), BF16), vm((2, n_dz, rows, PAIR), BF16),
         vm((rows, hid), F32), vm((2 * rows, att), BF16),
         vm((N_SEQ * rows, 2 * rows), F32), vm((N_SEQ * rows, 2 * rows), BF16),
         vm((width, 2 * hid), BF16), vm((width, 2 * att), BF16),
@@ -534,30 +628,30 @@
         vm((N_Z - 1, 2, chunk, rest_m), BF16), vm((chunk, rest_m), BF16),
         vm((half, cut_att), BF16), vm((N_Z - 1, chunk, cut_att), BF16),
         vm((N_Z - 1, 2, chunk, rest_a), BF16), vm((chunk, rest_a), BF16),
-        vm((chunk, 2 * hid), BF16), vm((chunk, 2 * att), BF16),
-        pltpu.SemaphoreType.DMA((7,)), pltpu.SemaphoreType.DMA((6,)),
+        vm((2, chunk, hid), BF16), vm((3, chunk, local), BF16), vm((chunk, local), BF16),
+        pltpu.SemaphoreType.DMA((9,)), pltpu.SemaphoreType.DMA((8,)),
         pltpu.SemaphoreType.DMA((N_COPIES,)), pltpu.SemaphoreType.DMA((N_COPIES,)),
     ]
     any_spec = pl.BlockSpec(memory_space=pl.ANY)
-    recon, gatt, gmlp = pl.pallas_call(
+    recon, grad_qkv, grad_out, grad_up, grad_down = pl.pallas_call(
         lambda *refs: kernel(sizes, *refs),
         out_shape=(
             jax.ShapeDtypeStruct((4, rows, width), F32),
-            jax.ShapeDtypeStruct((chunk, 2 * att), BF16),
-            jax.ShapeDtypeStruct((chunk, 2 * hid), BF16),
+            jax.ShapeDtypeStruct((3, chunk, local), BF16),
+            jax.ShapeDtypeStruct((chunk, local), BF16),
+            jax.ShapeDtypeStruct((chunk, hid), BF16),
+            jax.ShapeDtypeStruct((chunk, hid), BF16),
         ),
         in_specs=[any_spec] * 7,
-        out_specs=(any_spec,) * 3,
+        out_specs=(any_spec,) * 5,
         scratch_shapes=scratch,
         compiler_params=pltpu.CompilerParams(
             collective_id=0, has_side_effects=True, vmem_limit_bytes=67043328
         ),
         name="window",
-    )(streams[0], head_streams, gains[0], wkv, wqo, w_up[0], w_down[0])
-    pairs = gatt.reshape(chunk, 2, heads, 2, HEAD_DIM)
-    grad_qkv = jnp.stack([pairs[:, 1, :, 0], pairs[:, 0, :, 0], pairs[:, 0, :, 1]], 1).reshape(chunk, 3, local)
-    grad_out = pairs[:, 1, :, 1].reshape(chunk, local)
-    return (recon[None], grad_qkv[None], grad_out[None], gmlp[None, :, :hid], gmlp[None, :, hid:])
+    )(streams[0], head_streams, gains[0], wqkv, wout, w_up[0], w_down[0])
+    grad_qkv = jnp.transpose(grad_qkv, (1, 0, 2))
+    return (recon[None], grad_qkv[None], grad_out[None], grad_up[None], grad_down[None])
 
 
 def solution(mesh):

time: 230 us -> 209 us (0.909)
  Pallas kernels: 213 us -> 202 us
  local copies, waits for them, and re-layouts: 13.5 us -> 6.49 us
    pallas_call x1, Pallas kernels: 213 us -> 202 us  [per_device(): pl.pallas_call(lambda *refs: kernel(sizes, *refs), out_shape=(jax.ShapeDt...]
    reshape x2 -> x0, local copies, waits for them, and re-layouts: 4.37 us -> none  [the longest x1 2.19 us: per_device(): wkv = jnp.stack([parts[:, 1], parts[:, 2]], 2).reshape(width, att)]
    unnamed x7 -> x13, local copies, waits for them, and re-layouts: 3.22 us -> 6.49 us
where the time goes in v2:
time: 209 us
  Pallas kernels  202 us (97%)
  local copies, waits for them, and re-layouts  6.49 us (3%)
    pallas_call x1, Pallas kernels, per_device(): pl.pallas_call(lambda *refs: kernel(sizes, *refs), out_shape=(jax.ShapeDt...  202 us
    unnamed x13, local copies, waits for them, and re-layouts  6.49 us

profile of v2, /device:TPU:1, one launch (start us, length us, event | category | flops | bytes accessed | tf_op | source)
XLA Modules:
  0.0 208.7 jit_solution(7868937853667676903)
XLA Ops:
  0.6 201.6 %window.1 = (f32[4,128,1280]{2,1,0:T(8,128)}, bf16[3,160,320]{2,1,0:T(8,128)(2,1)}, bf16[160,320]{1,0:T(8,128)(2,1)}, bf16[160,1280]{1,0:T(8,128)(2,1)}, bf16[160,1280]{1,0:T(8,128)(2,1)}) custom-call(f32[4,128,1280]{2,1,0:T(8,128)} %bitcast.23, f32[4,128,1280]{2,1,0:T(8,128)} %refs_1_.1, f32[2,1280]{1,0:T(2,128)} %bitcast.31, ...), custom_call_target="tpu_custom_call" | custom-call | tf_op jit(solution)/shard_map/window/pallas_call | solution.py:636
  202.2 0.0 copy-start.2
  202.2 0.0 copy-start.3
  202.2 0.0 copy-start.1
  202.2 0.0 copy-start
  202.3 3.6 %copy.17 = f32[1,4,128,1280]{3,2,1,0:T(8,128)} copy(f32[1,4,128,1280]{3,2,1,0:T(8,128)} %bitcast.24) | data formatting | bytes 5242880
  205.8 0.0 copy-done.2
  205.8 0.7 copy.18
  206.6 0.0 copy-done.3
  206.6 0.6 copy.19
  207.2 0.0 copy-done.1
  207.2 0.8 copy.20
  208.0 0.0 copy-done
  208.0 0.8 copy.21
Async XLA Ops:
  202.2 3.6 %copy-start.2 = (bf16[3,160,320]{2,1,0:T(8,128)(2,1)S(1)}, bf16[3,160,320]{2,1,0:T(8,128)(2,1)}, u32[]{:S(2)}) copy-start(bf16[3,160,320]{2,1,0:T(8,128)(2,1)} %get-tuple-element.11) | copy-start | bytes 921604
  202.2 4.4 %copy-start.3 = (bf16[160,320]{1,0:T(8,128)(2,1)S(1)}, bf16[160,320]{1,0:T(8,128)(2,1)}, u32[]{:S(2)}) copy-start(bf16[160,320]{1,0:T(8,128)(2,1)} %get-tuple-element.12) | copy-start | bytes 307204
  202.2 5.0 %copy-start.1 = (bf16[160,1280]{1,0:T(8,128)(2,1)S(1)}, bf16[160,1280]{1,0:T(8,128)(2,1)}, u32[]{:S(2)}) copy-start(bf16[160,1280]{1,0:T(8,128)(2,1)} %get-tuple-element.13) | copy-start | bytes 1228804
  202.2 5.7 %copy-start = (bf16[160,1280]{1,0:T(8,128)(2,1)S(1)}, bf16[160,1280]{1,0:T(8,128)(2,1)}, u32[]{:S(2)}) copy-start(bf16[160,1280]{1,0:T(8,128)(2,1)} %get-tuple-element.14) | copy-start | bytes 1228804

commit v3 on v2

--- a/solution.py
+++ b/solution.py
@@ -18,6 +18,7 @@
 N_SEC = 4
 KV_X_FIRST = 2
 DKV_X_FIRST = 3
+HIDDEN_X_FIRST = 768
 NU, GL, AL, TL = 0, 1, 2, 3
 NN = (((1,), (0,)), ((), ()))
 NT = (((1,), (1,)), ((), ()))
@@ -95,9 +96,10 @@
     (recon_h, gqkv_h, gout_h, gup_h, gdn_h) = refs[7:12]
     (
         xs, hd, gains, wkv, wqo, wup, wdn,
-        rx, sx, fl, gp, hidden, dkvf, dqf, mxf,
+        rx, sx, fl, gp, hall, glt, gsl, dkvf, dqf, mxf,
         snd, rr, ag, kvb, dks, dax, daz, dbz, dbx, pre, qd, scores, pd,
-        gmlp, gatt, ra_m, rz_m, rb_m, rw_m, ra_a, rz_a, rb_a, rw_a, om, oqkv, oout,
+        gmlp, gatt, gkv, ra_m, rz_m, rb_m, rw_m, ra_a, rz_a, rb_a, rw_a,
+        ra_k, rz_k, rb_k, rw_k, om, oqkv, oout,
         load_sem, out_sem, send_sem, recv_sem,
     ) = refs[12:]
     heads = att // PAIR
@@ -130,17 +132,21 @@
     for d in range(N_TP):
         pl.semaphore_signal(barrier, inc=1, device_id=sec_dev(1, d), device_id_type=MESH)
 
+    moves = (
+        (gains_h, gains), (streams_h.at[0], xs.at[0]), (wup_h, wup), (wdn_h, wdn),
+        (streams_h.at[3], xs.at[3]), (streams_h.at[1], xs.at[1]), (streams_h.at[2], xs.at[2]),
+        (wqkv_h.at[1], wkv.at[:, 0]), (wqkv_h.at[2], wkv.at[:, 1]),
+        (wqkv_h.at[0], wqo.at[:, 0]), (wout_h, wqo.at[:, 1]), (head_h, hd),
+    )
     loads = []
-    for k, (src, dst) in enumerate(
-        (
-            (streams_h, xs), (gains_h, gains), (wup_h, wup), (wdn_h, wdn),
-            (wqkv_h.at[1], wkv.at[:, 0]), (wqkv_h.at[2], wkv.at[:, 1]),
-            (wqkv_h.at[0], wqo.at[:, 0]), (wout_h, wqo.at[:, 1]), (head_h, hd),
-        )
-    ):
-        copy = pltpu.make_async_copy(src, dst, load_sem.at[k])
-        copy.start()
-        loads.append(copy)
+
+    def load(count):
+        for src, dst in moves[len(loads) : len(loads) + count]:
+            copy = pltpu.make_async_copy(src, dst, load_sem.at[len(loads)])
+            copy.start()
+            loads.append(copy)
+
+    load(5)
     sender = Sender(send_sem, recv_sem)
 
     lane = lax.broadcasted_iota(jnp.int32, (rows, PAIR), 1)
@@ -188,14 +194,14 @@
         def up(c):
             out = dot(fl[NU, pl.ds(t * rows, rows), :], wup[:, pl.ds(c, 256)], NN)
             pre[:, pl.ds(c, 256)] = out
-            hidden[pl.ds(t * rows, rows), pl.ds(c, 256)] = gelu(out).astype(BF16)
+            hall[t, 0, 0, :, pl.ds(c, 256)] = gelu(out).astype(BF16)
 
         loop(hid // 256, 256, up)
 
     def mlp_down(t):
         def down(c):
             snd[t, 0, :, pl.ds(c, 256)] = dot(
-                hidden[pl.ds(t * rows, rows), :], wdn[pl.ds(c, 256), :], NT
+                hall[t, 0, 0], wdn[pl.ds(c, 256), :], NT
             ).astype(BF16)
 
         loop(width // 256, 256, down)
@@ -220,6 +226,56 @@
             ).astype(BF16)
 
         loop(width // 256, 256, out)
+
+    def share(ref, t, cut):
+        own, size = ref.at[t, 0, 0], ref.shape[4]
+        left, right = pl.ds(0, cut), pl.ds(cut, size - cut)
+        across = sender.start(own.at[:, left], ref.at[t, 1, 0, :, left], seq_dev(N_Z))
+        along = [sender.start(own, ref.at[t, 0, d], seq_dev(d)) for d in range(1, N_Z)]
+        rest = sender.start(own.at[:, right], ref.at[t, 1, 0, :, right], seq_dev(N_Z))
+        return across, along, rest
+
+    def share_pass(ref, t, cut, copies):
+        across, along, rest = copies
+        left, right = pl.ds(0, cut), pl.ds(cut, ref.shape[4] - cut)
+        received([across])
+        late = [
+            sender.start(ref.at[t, 1, 0, :, left], ref.at[t, 1, d, :, left], seq_dev(d))
+            for d in range(1, N_Z)
+        ]
+        received(along)
+        late += [
+            sender.start(ref.at[t, 0, d, :, right], ref.at[t, 1, d, :, right], seq_dev(N_Z))
+            for d in range(1, N_Z)
+        ]
+        return late + [rest]
+
+    def slices_out(t, factor, turned, gathered):
+        def turn(c):
+            tile = fl[factor, pl.ds(t * rows, rows), pl.ds(c, 128)]
+            turned[t, pl.ds(c, 128), :] = tile.astype(F32).T.astype(BF16)
+
+        loop(width // 128, 128, turn)
+        gathered[:, pl.ds(t * N_SEQ * rows, rows)] = turned[t, grad_rows(0, 0), :]
+        return [
+            sender.start(
+                turned.at[t, grad_rows(d // N_Z, d % N_Z), :],
+                gathered.at[:, pl.ds((t * N_SEQ + d) * rows, rows)],
+                seq_dev(d),
+            )
+            for d in range(1, N_SEQ)
+        ]
+
+    def grads_down(copies):
+        received(copies)
+
+        def tile(c):
+            cols = pl.ds(c, 256)
+            om[1, :, cols] = dot(
+                gsl[...], hall[:, :, :, :, cols].reshape(2 * N_SEQ * rows, 256), NN
+            ).astype(BF16)
+
+        loop(hid // 256, 256, tile)
 
     def attention_in(t, x, slot):
         gain = gains[0:1, :]
@@ -426,60 +482,69 @@
         loop(chunk // 32, 32, add)
 
     def store_mlp(here, left, right):
-        om[0, here, :] = left[:, :hid]
-        om[1, here, pl.ds(0, cut_mlp - hid)] = left[:, hid:]
-        om[1, here, pl.ds(cut_mlp - hid, 2 * hid - cut_mlp)] = right
-
-    def store_att(here, left, right):
-        def piece(p, h, k):
-            start = p * att + h * PAIR + k * HEAD_DIM
+        om[0, here, pl.ds(0, cut_mlp)] = left
+        om[0, here, pl.ds(cut_mlp, hid - cut_mlp)] = right
+
+    def joined(left, right, k):
+        pieces = []
+        for h in range(heads):
+            start = h * PAIR + k * HEAD_DIM
             if start < cut_att:
-                return left[:, start : start + HEAD_DIM]
-            return right[:, start - cut_att : start - cut_att + HEAD_DIM]
-
-        def joined(p, k):
-            return jnp.concatenate([piece(p, h, k) for h in range(heads)], 1)
-
-        oqkv[0, here, :] = joined(1, 0)
-        oqkv[1, here, :] = joined(0, 0)
-        oqkv[2, here, :] = joined(0, 1)
-        oout[here, :] = joined(1, 1)
+                pieces.append(left[:, start : start + HEAD_DIM])
+            else:
+                pieces.append(right[:, start - cut_att : start - cut_att + HEAD_DIM])
+        return jnp.concatenate(pieces, 1)
+
+    def store_qo(here, left, right):
+        oqkv[0, here, :] = joined(left, right, 0)
+        oout[here, :] = joined(left, right, 1)
+
+    def store_kv(here, left, right):
+        oqkv[1, here, :] = joined(left, right, 0)
+        oqkv[2, here, :] = joined(left, right, 1)
 
     def grads_mlp():
         def tile(c):
-            gmlp[pl.ds(c, 256), pl.ds(0, hid)] = dot(fl[NU, :, pl.ds(c, 256)], gp[...], TN).astype(BF16)
-            gmlp[pl.ds(c, 256), pl.ds(hid, hid)] = dot(fl[GL, :, pl.ds(c, 256)], hidden[...], TN).astype(BF16)
+            gmlp[pl.ds(c, 256), :] = dot(fl[NU, :, pl.ds(c, 256)], gp[...], TN).astype(BF16)
 
         loop(width // 256, 256, tile)
         return reduce_first(gmlp, cut_mlp, ra_m, rb_m)
 
     def grads_att():
         def tile(c):
-            left = fl[AL, :, pl.ds(c, 256)]
-            gatt[pl.ds(c, 256), pl.ds(0, att)] = dot(left, dkvf[...], TN).astype(BF16)
-            gatt[pl.ds(c, 256), pl.ds(att, att)] = (
-                dot(left, dqf[...], TN) + dot(fl[TL, :, pl.ds(c, 256)], mxf[...], TN)
+            gatt[pl.ds(c, 256), :] = (
+                dot(fl[AL, :, pl.ds(c, 256)], dqf[...], TN) + dot(fl[TL, :, pl.ds(c, 256)], mxf[...], TN)
             ).astype(BF16)
 
         loop(width // 256, 256, tile)
         return reduce_first(gatt, cut_att, ra_a, rb_a)
+
+    def grads_kv():
+        def tile(c):
+            gkv[pl.ds(c, 256), :] = dot(fl[AL, :, pl.ds(c, 256)], dkvf[...], TN).astype(BF16)
+
+        loop(width // 256, 256, tile)
+        return reduce_first(gkv, cut_att, ra_k, rb_k)
 
     loads[0].wait()
     loads[1].wait()
     mlp_forward(0, xs)
     loads[2].wait()
     mlp_hidden(0)
+    pl.semaphore_wait(barrier, N_TP - 1 + N_SEQ - 1 + N_TP)
+    c_hid = share(hall, 0, HIDDEN_X_FIRST)
     loads[3].wait()
+    load(7)
     mlp_down(0)
-    pl.semaphore_wait(barrier, N_TP - 1 + N_SEQ - 1 + N_TP)
-    c_mlp = scatter(0, 0)
+    c_mlp = c_first = scatter(0, 0)
+    loads[4].wait()
     mlp_back(0, xs)
     c_mlp = spread(0, summed(0, 0, c_mlp))
     received(c_mlp)
     c_grad = scatter(0, 1)
-    for k in range(4, 8):
+    for k in range(5, 11):
         loads[k].wait()
-    for copy in sender.all[:3]:
+    for copy in c_first:
         copy.wait_send()
     c_kv = attention_in(0, xs, 0)
     late = pass_along(0, c_kv)
@@ -493,9 +558,10 @@
     c_up = send_section(0, xs[0, mine, :] - summed(0, 2, c_att))
     c_low = sender.start(snd.at[0, 0], rx.at[1], sec_dev(N_SEC - 1, 0))
     c_total = sender.start(fl.at[TL, pl.ds(0, rows), :], rx.at[2], sec_dev(N_SEC - 1, 0))
+    c_down = share_pass(hall, 0, HIDDEN_X_FIRST, c_hid) + slices_out(0, GL, glt, gsl)
 
     is_last = sec == N_SEC - 1
-    loads[8].wait()
+    loads[11].wait()
 
     def choose(k):
         def one(r):
@@ -525,6 +591,7 @@
     mlp_hidden(1)
     mlp_down(1)
     c_mlp = scatter(1, 0)
+    c_hid = share(hall, 1, HIDDEN_X_FIRST)
     grad = summed(0, 3, c_att)
     c_gl = send_section(1, xs[3, mine, :] + norm_back(grad, slope, xs[1, mine, :]))
     c_mlp = spread(2, summed(1, 0, c_mlp))
@@ -535,24 +602,28 @@
     emit(1)
     received(c_gl)
     choose(3)
-    late = pass_across(1, c_kv, pass_along(1, c_kv))
     mlp_back(1, hd)
     c_grad = scatter(1, 1)
+    late = pass_along(1, c_kv)
     c_gm = grads_mlp()
+    late = pass_across(1, c_kv, late)
     c_grad = spread(3, summed(1, 1, c_grad))
     received([c_total])
     choose(2)
+    c_down += slices_out(1, GL, glt, gsl)
+    c_down += share_pass(hall, 1, HIDDEN_X_FIRST, c_hid)
     received(c_grad)
     grads_in(1, hd, 3)
     emit(2)
     c_dkv = attend(1, c_kv, late)
     c_att = attention_out(1)
     c_dkv = attention_relay(1, c_dkv)
+    c_gm = reduce_second(gmlp, cut_mlp, ra_m, rb_m, rz_m, rw_m, c_gm)
+    c_ga = grads_att()
     c_up = spread(4, summed(1, 2, c_att))
     c_att = attention_back(1, c_dkv)
-    c_ga = grads_att()
+    c_gk = grads_kv()
     c_gl = spread(5, summed(1, 3, c_att))
-    c_gm = reduce_second(gmlp, cut_mlp, ra_m, rb_m, rz_m, rw_m, c_gm)
     received(c_up)
 
     def upper(r):
@@ -578,19 +649,22 @@
     loop(rows // 32, 32, lower)
     emit(3)
     c_ga = reduce_second(gatt, cut_att, ra_a, rb_a, rz_a, rw_a, c_ga)
+    grads_down(c_down)
+    finish(om.at[1], gdn_h, 5)
     reduce_last(gmlp, cut_mlp, rz_m, rw_m, store_mlp, c_gm)
     finish(om.at[0], gup_h, 4)
-    finish(om.at[1], gdn_h, 5)
-    reduce_last(gatt, cut_att, rz_a, rw_a, store_att, c_ga)
+    c_gk = reduce_second(gkv, cut_att, ra_k, rb_k, rz_k, rw_k, c_gk)
+    reduce_last(gatt, cut_att, rz_a, rw_a, store_qo, c_ga)
+    finish(oout, gout_h, 7)
+    reduce_last(gkv, cut_att, rz_k, rw_k, store_kv, c_gk)
     finish(oqkv, gqkv_h, 6)
-    finish(oout, gout_h, 7)
-    for copy in sender.all[3:]:
+    for copy in [c for c in sender.all if all(c is not f for f in c_first)]:
         copy.wait_send()
     for copy in outs:
         copy.wait()
 
 
-N_COPIES = 240
+N_COPIES = 312
 
 
 def per_device(streams, head_streams, gains, w_qkv, w_out, w_up, w_down):
@@ -601,13 +675,13 @@
     heads = local // HEAD_DIM
     chunk = width // N_SEQ
     half = width // 2
-    cut_mlp = 1536
-    cut_att = 768
+    cut_mlp = 768
+    cut_att = 384
     wqkv = jnp.transpose(w_qkv[0], (1, 2, 0)).reshape(3, heads, HEAD_DIM, width)
     wout = jnp.transpose(w_out[0], (1, 0)).reshape(heads, HEAD_DIM, width)
     sizes = (rows, width, hid, att, cut_mlp, cut_att)
     quarter = rows // N_TP
-    rest_m, rest_a = 2 * hid - cut_mlp, 2 * att - cut_att
+    rest_m, rest_a = hid - cut_mlp, att - cut_att
     n_dx, n_dz = DKV_X_FIRST, heads - DKV_X_FIRST
     vm = pltpu.VMEM
     scratch = [
@@ -615,7 +689,8 @@
         vm((heads, 2, HEAD_DIM, width), BF16), vm((heads, 2, HEAD_DIM, width), BF16),
         vm((width, hid), BF16), vm((width, hid), BF16),
         vm((4, rows, width), BF16), vm((2, quarter, width), BF16),
-        vm((4, 2 * rows, width), BF16), vm((2 * rows, hid), BF16), vm((2 * rows, hid), BF16),
+        vm((4, 2 * rows, width), BF16), vm((2 * rows, hid), BF16),
+        vm((2, 2, N_Z, rows, hid), BF16), vm((2, width, rows), BF16), vm((chunk, 2 * N_SEQ * rows), BF16),
         vm((2 * rows, att), BF16), vm((2 * rows, att), BF16), vm((2 * rows, att), BF16),
         vm((2, 4, rows, width), BF16), vm((2, 4, N_TP - 1, quarter, width), BF16), vm((6, rows, width), BF16),
         vm((2, heads, 2, N_Z, rows, PAIR), BF16), vm((2, heads, 2, N_Z, rows, PAIR), BF16),
@@ -623,13 +698,15 @@
         vm((2, n_dz, N_Z - 1, 2, rows, PAIR), BF16), vm((2, n_dz, rows, PAIR), BF16),
         vm((rows, hid), F32), vm((2 * rows, att), BF16),
         vm((N_SEQ * rows, 2 * rows), F32), vm((N_SEQ * rows, 2 * rows), BF16),
-        vm((width, 2 * hid), BF16), vm((width, 2 * att), BF16),
+        vm((width, hid), BF16), vm((width, att), BF16), vm((width, att), BF16),
         vm((half, cut_mlp), BF16), vm((N_Z - 1, chunk, cut_mlp), BF16),
         vm((N_Z - 1, 2, chunk, rest_m), BF16), vm((chunk, rest_m), BF16),
         vm((half, cut_att), BF16), vm((N_Z - 1, chunk, cut_att), BF16),
         vm((N_Z - 1, 2, chunk, rest_a), BF16), vm((chunk, rest_a), BF16),
+        vm((half, cut_att), BF16), vm((N_Z - 1, chunk, cut_att), BF16),
+        vm((N_Z - 1, 2, chunk, rest_a), BF16), vm((chunk, rest_a), BF16),
         vm((2, chunk, hid), BF16), vm((3, chunk, local), BF16), vm((chunk, local), BF16),
-        pltpu.SemaphoreType.DMA((9,)), pltpu.SemaphoreType.DMA((8,)),
+        pltpu.SemaphoreType.DMA((12,)), pltpu.SemaphoreType.DMA((8,)),
         pltpu.SemaphoreType.DMA((N_COPIES,)), pltpu.SemaphoreType.DMA((N_COPIES,)),
     ]
     any_spec = pl.BlockSpec(memory_space=pl.ANY)

time: 209 us -> 191 us (0.914)
  Pallas kernels: 202 us -> 184 us
    pallas_call x1, Pallas kernels: 202 us -> 184 us  [per_device(): pl.pallas_call(lambda *refs: kernel(sizes, *refs), out_shape=(jax.ShapeDt...]
where the time goes in v3:
time: 191 us
  Pallas kernels  184 us (96%)
  local copies, waits for them, and re-layouts  6.49 us (3%)
    pallas_call x1, Pallas kernels, per_device(): pl.pallas_call(lambda *refs: kernel(sizes, *refs), out_shape=(jax.ShapeDt...  184 us
    unnamed x13, local copies, waits for them, and re-layouts  6.49 us

profile of v3, /device:TPU:1, one launch (start us, length us, event | category | flops | bytes accessed | tf_op | source)
XLA Modules:
  0.0 191.1 jit_solution(10807059947854407907)
XLA Ops:
  0.6 183.9 %window.1 = (f32[4,128,1280]{2,1,0:T(8,128)}, bf16[3,160,320]{2,1,0:T(8,128)(2,1)}, bf16[160,320]{1,0:T(8,128)(2,1)}, bf16[160,1280]{1,0:T(8,128)(2,1)}, bf16[160,1280]{1,0:T(8,128)(2,1)}) custom-call(f32[4,128,1280]{2,1,0:T(8,128)} %bitcast.23, f32[4,128,1280]{2,1,0:T(8,128)} %refs_1_.1, f32[2,1280]{1,0:T(2,128)} %bitcast.31, ...), custom_call_target="tpu_custom_call" | custom-call | tf_op jit(solution)/shard_map/window/pallas_call | solution.py:713
  184.6 0.0 copy-start.2
  184.6 0.0 copy-start.3
  184.6 0.0 copy-start.1
  184.6 0.0 copy-start
  184.6 3.6 %copy.17 = f32[1,4,128,1280]{3,2,1,0:T(8,128)} copy(f32[1,4,128,1280]{3,2,1,0:T(8,128)} %bitcast.24) | data formatting | bytes 5242880
  188.2 0.0 copy-done.2
  188.2 0.7 copy.18
  188.9 0.0 copy-done.3
  188.9 0.6 copy.19
  189.6 0.0 copy-done.1
  189.6 0.8 copy.20
  190.3 0.0 copy-done
  190.3 0.8 copy.21
Async XLA Ops:
  184.6 3.6 %copy-start.2 = (bf16[3,160,320]{2,1,0:T(8,128)(2,1)S(1)}, bf16[3,160,320]{2,1,0:T(8,128)(2,1)}, u32[]{:S(2)}) copy-start(bf16[3,160,320]{2,1,0:T(8,128)(2,1)} %get-tuple-element.11) | copy-start | bytes 921604
  184.6 4.4 %copy-start.3 = (bf16[160,320]{1,0:T(8,128)(2,1)S(1)}, bf16[160,320]{1,0:T(8,128)(2,1)}, u32[]{:S(2)}) copy-start(bf16[160,320]{1,0:T(8,128)(2,1)} %get-tuple-element.12) | copy-start | bytes 307204
  184.6 5.0 %copy-start.1 = (bf16[160,1280]{1,0:T(8,128)(2,1)S(1)}, bf16[160,1280]{1,0:T(8,128)(2,1)}, u32[]{:S(2)}) copy-start(bf16[160,1280]{1,0:T(8,128)(2,1)} %get-tuple-element.13) | copy-start | bytes 1228804
  184.6 5.7 %copy-start = (bf16[160,1280]{1,0:T(8,128)(2,1)S(1)}, bf16[160,1280]{1,0:T(8,128)(2,1)}, u32[]{:S(2)}) copy-start(bf16[160,1280]{1,0:T(8,128)(2,1)} %get-tuple-element.14) | copy-start | bytes 1228804

commit v4 on v3

--- a/solution.py
+++ b/solution.py
@@ -98,8 +98,8 @@
         xs, hd, gains, wkv, wqo, wup, wdn,
         rx, sx, fl, gp, hall, glt, gsl, dkvf, dqf, mxf,
         snd, rr, ag, kvb, dks, dax, daz, dbz, dbx, pre, qd, scores, pd,
-        gmlp, gatt, gkv, ra_m, rz_m, rb_m, rw_m, ra_a, rz_a, rb_a, rw_a,
-        ra_k, rz_k, rb_k, rw_k, om, oqkv, oout,
+        gmlp, gatt, gkv, xa_m, pa_m, fa_m, pb_m, fb_m, xb_m, xa_a, pa_a, fa_a, pb_a, fb_a, xb_a,
+        xa_k, pa_k, fa_k, pb_k, fb_k, xb_k, om, oqkv, oout,
         load_sem, out_sem, send_sem, recv_sem,
     ) = refs[12:]
     heads = att // PAIR
@@ -181,6 +181,12 @@
             for d in range(N_TP)
         ]
 
+    def section_spread(k, copy):
+        received([copy])
+        return [
+            sender.start(rx.at[k, mine, :], rx.at[k, mine, :], tp_dev(d)) for d in range(1, N_TP)
+        ]
+
     def mlp_forward(t, x):
         gain = gains[1:2, :]
 
@@ -228,12 +234,17 @@
         loop(width // 256, 256, out)
 
     def share(ref, t, cut):
-        own, size = ref.at[t, 0, 0], ref.shape[4]
-        left, right = pl.ds(0, cut), pl.ds(cut, size - cut)
+        own, left = ref.at[t, 0, 0], pl.ds(0, cut)
         across = sender.start(own.at[:, left], ref.at[t, 1, 0, :, left], seq_dev(N_Z))
-        along = [sender.start(own, ref.at[t, 0, d], seq_dev(d)) for d in range(1, N_Z)]
+        along = [sender.start(own, ref.at[t, 0, d], seq_dev(d)) for d in (1, 3)]
+        return across, along
+
+    def share_rest(ref, t, cut, copies):
+        across, along = copies
+        own, right = ref.at[t, 0, 0], pl.ds(cut, ref.shape[4] - cut)
+        far = sender.start(own, ref.at[t, 0, 2], seq_dev(2))
         rest = sender.start(own.at[:, right], ref.at[t, 1, 0, :, right], seq_dev(N_Z))
-        return across, along, rest
+        return across, along + [far], rest
 
     def share_pass(ref, t, cut, copies):
         across, along, rest = copies
@@ -257,6 +268,8 @@
 
         loop(width // 128, 128, turn)
         gathered[:, pl.ds(t * N_SEQ * rows, rows)] = turned[t, grad_rows(0, 0), :]
+
+    def slices_send(t, turned, gathered):
         return [
             sender.start(
                 turned.at[t, grad_rows(d // N_Z, d % N_Z), :],
@@ -366,7 +379,7 @@
                         for d in range(1, N_Z)
                     ]
                 )
-            mixed = dot(pd[...], kv, TN)
+            mixed = dot(kv, pd[...], TN).T
             dqf[pl.ds(t * rows, rows), lanes] = jnp.where(lane < HEAD_DIM, mixed[:rows] * 0.125, 0.0).astype(BF16)
             mxf[pl.ds(t * rows, rows), lanes] = jnp.where(lane >= HEAD_DIM, mixed[rows:], 0.0).astype(BF16)
         return first
@@ -426,60 +439,96 @@
         index = lax.rem(x_hi + by_x, 2) * N_Z + lax.rem(z + by_z, N_Z)
         return pl.ds(pl.multiple_of(index * chunk, 32), chunk)
 
-    def reduce_first(g, cut, ra, rb):
-        other = pl.ds(pl.multiple_of((1 - x_hi) * half, 32), half)
-        cols_a, cols_b = pl.ds(0, cut), pl.ds(cut, g.shape[1] - cut)
-        first = [sender.start(g.at[other, cols_a], ra, seq_dev(N_Z))]
-        second = []
-        for d in range(1, N_Z):
-            for k in range(2):
-                second.append(sender.start(g.at[grad_rows(k, d), cols_b], rb.at[d - 1, k], seq_dev(d)))
-        return first, second
-
-    def reduce_second(g, cut, ra, rb, rz, rw, copies):
-        first, second = copies
-        cols_a, cols_b = pl.ds(0, cut), pl.ds(cut, g.shape[1] - cut)
-        base = x_hi * half
-        received(first)
-
-        def add_a(r):
-            here = pl.ds(pl.multiple_of(base + r, 32), 32)
-            g[here, cols_a] = (g[here, cols_a].astype(F32) + ra[pl.ds(r, 32), :].astype(F32)).astype(BF16)
-
-        loop(half // 32, 32, add_a)
-        out = [
-            sender.start(g.at[grad_rows(0, d), cols_a], rz.at[d - 1], seq_dev(d)) for d in range(1, N_Z)
-        ]
-        received(second)
-        for k in (1, 0):
-            start = (lax.rem(x_hi + k, 2) * N_Z + z) * chunk
-
-            def add_b(r):
-                here = pl.ds(pl.multiple_of(start + r, 32), 32)
-                total = g[here, cols_b].astype(F32)
-                for d in range(N_Z - 1):
-                    total = total + rb[d, k, pl.ds(r, 32), :].astype(F32)
-                g[here, cols_b] = total.astype(BF16)
-
-            loop(chunk // 32, 32, add_b)
-            if k == 1:
-                out.append(sender.start(g.at[grad_rows(1, 0), cols_b], rw, seq_dev(N_Z)))
-        return out
-
-    def reduce_last(g, cut, rz, rw, store, copies):
-        cols_a, cols_b = pl.ds(0, cut), pl.ds(cut, g.shape[1] - cut)
-        received(copies)
-        start = seq * chunk
-
+    part = chunk // 2
+
+    def part_rows(by_x, by_z, side):
+        index = lax.rem(x_hi + by_x, 2) * N_Z + lax.rem(z + by_z, N_Z)
+        return index * chunk + side * part
+
+    def add_rows(g, cols, start, count, *terms):
         def add(r):
-            here = pl.ds(pl.multiple_of(start + r, 32), 32)
-            total = g[here, cols_a].astype(F32)
-            for d in range(N_Z - 1):
-                total = total + rz[d, pl.ds(r, 32), :].astype(F32)
-            rest = g[here, cols_b].astype(F32) + rw[pl.ds(r, 32), :].astype(F32)
-            store(pl.ds(r, 32), total.astype(BF16), rest.astype(BF16))
-
-        loop(chunk // 32, 32, add)
+            here = pl.ds(pl.multiple_of(start + r, 16), 16)
+            total = g[here, cols].astype(F32)
+            for term in terms:
+                total = total + term(pl.ds(r, 16)).astype(F32)
+            g[here, cols] = total.astype(BF16)
+
+        loop(count // 16, 16, add)
+
+    def ring_start(g, cols, ks, pass_buf, final):
+        def ship(k, d, side, dst, to):
+            rows_at = pl.ds(pl.multiple_of(part_rows(k, d, side), 16), part)
+            return sender.start(g.at[rows_at, cols], dst, seq_dev(to))
+
+        up = [ship(k, 2, 0, pass_buf.at[0, i], 1) for i, k in enumerate(ks)]
+        down = [ship(k, 2, 1, pass_buf.at[1, i], 3) for i, k in enumerate(ks)]
+        rest = []
+        for i, k in enumerate(ks):
+            rest.append(ship(k, 1, 1, final.at[0, i, pl.ds(part, part)], 1))
+            rest.append(ship(k, 3, 0, final.at[1, i, pl.ds(0, part)], 3))
+        return up, down, rest
+
+    def ring_relay(g, cols, ks, pass_buf, final, copies):
+        up, down, rest = copies
+        for i, k in enumerate(ks):
+            for group, d, side in ((up, 1, 0), (down, 3, 1)):
+                received([group[i]])
+                start = part_rows(k, d, side)
+                add_rows(g, cols, start, part, lambda here, side=side: pass_buf[side, i, here, :])
+                rows_at = pl.ds(pl.multiple_of(start, 16), part)
+                rest.append(
+                    sender.start(g.at[rows_at, cols], final.at[side, i, pl.ds(side * part, part)], seq_dev(d))
+                )
+        return rest
+
+    class Reduction:
+        def __init__(self, g, cut, xa, pa, fa, pb, fb, xb):
+            self.g, self.xa, self.pa, self.fa, self.pb, self.fb, self.xb = g, xa, pa, fa, pb, fb, xb
+            self.cols_a, self.cols_b = pl.ds(0, cut), pl.ds(cut, g.shape[1] - cut)
+
+        def first(self):
+            other = pl.ds(pl.multiple_of((1 - x_hi) * half, 32), half)
+            self.across = [sender.start(self.g.at[other, self.cols_a], self.xa, seq_dev(N_Z))]
+            self.ring_b = ring_start(self.g, self.cols_b, (1, 0), self.pb, self.fb)
+
+        def second_b(self):
+            self.rest_b = ring_relay(self.g, self.cols_b, (1, 0), self.pb, self.fb, self.ring_b)
+
+        def second_a(self):
+            received(self.across)
+            add_rows(self.g, self.cols_a, x_hi * half, half, lambda here: self.xa[here, :])
+            self.ring_a = ring_start(self.g, self.cols_a, (0,), self.pa, self.fa)
+
+        def third(self):
+            self.rest_a = ring_relay(self.g, self.cols_a, (0,), self.pa, self.fa, self.ring_a)
+            received(self.rest_b)
+            for i, k in enumerate((1, 0)):
+                add_rows(
+                    self.g, self.cols_b, part_rows(k, 0, 0), chunk,
+                    lambda here, i=i: self.fb[0, i, here, :], lambda here, i=i: self.fb[1, i, here, :],
+                )
+                if k == 1:
+                    rows_at = pl.ds(pl.multiple_of(part_rows(1, 0, 0), 16), chunk)
+                    self.back = [sender.start(self.g.at[rows_at, self.cols_b], self.xb, seq_dev(N_Z))]
+
+        def last(self, store):
+            received(self.rest_a)
+            received(self.back)
+            start = seq * chunk
+
+            def add(r):
+                here, out = pl.ds(pl.multiple_of(start + r, 32), 32), pl.ds(r, 32)
+                left = self.g[here, self.cols_a].astype(F32)
+                for k in range(2):
+                    left = left + self.fa[k, 0, out, :].astype(F32)
+                right = self.g[here, self.cols_b].astype(F32) + self.xb[out, :].astype(F32)
+                store(out, left.astype(BF16), right.astype(BF16))
+
+            loop(chunk // 32, 32, add)
+
+    red_m = Reduction(gmlp, cut_mlp, xa_m, pa_m, fa_m, pb_m, fb_m, xb_m)
+    red_a = Reduction(gatt, cut_att, xa_a, pa_a, fa_a, pb_a, fb_a, xb_a)
+    red_k = Reduction(gkv, cut_att, xa_k, pa_k, fa_k, pb_k, fb_k, xb_k)
 
     def store_mlp(here, left, right):
         om[0, here, pl.ds(0, cut_mlp)] = left
@@ -508,7 +557,6 @@
             gmlp[pl.ds(c, 256), :] = dot(fl[NU, :, pl.ds(c, 256)], gp[...], TN).astype(BF16)
 
         loop(width // 256, 256, tile)
-        return reduce_first(gmlp, cut_mlp, ra_m, rb_m)
 
     def grads_att():
         def tile(c):
@@ -517,28 +565,29 @@
             ).astype(BF16)
 
         loop(width // 256, 256, tile)
-        return reduce_first(gatt, cut_att, ra_a, rb_a)
+        red_a.first()
 
     def grads_kv():
         def tile(c):
             gkv[pl.ds(c, 256), :] = dot(fl[AL, :, pl.ds(c, 256)], dkvf[...], TN).astype(BF16)
 
         loop(width // 256, 256, tile)
-        return reduce_first(gkv, cut_att, ra_k, rb_k)
+        red_k.first()
 
     loads[0].wait()
     loads[1].wait()
     mlp_forward(0, xs)
     loads[2].wait()
     mlp_hidden(0)
-    pl.semaphore_wait(barrier, N_TP - 1 + N_SEQ - 1 + N_TP)
-    c_hid = share(hall, 0, HIDDEN_X_FIRST)
     loads[3].wait()
     load(7)
     mlp_down(0)
+    pl.semaphore_wait(barrier, N_TP - 1 + N_SEQ - 1 + N_TP)
     c_mlp = c_first = scatter(0, 0)
+    c_hid = share(hall, 0, HIDDEN_X_FIRST)
     loads[4].wait()
     mlp_back(0, xs)
+    slices_out(0, GL, glt, gsl)
     c_mlp = spread(0, summed(0, 0, c_mlp))
     received(c_mlp)
     c_grad = scatter(0, 1)
@@ -547,18 +596,23 @@
     for copy in c_first:
         copy.wait_send()
     c_kv = attention_in(0, xs, 0)
+    c_low = sender.start(snd.at[0, 0, mine, :], rx.at[1, mine, :], sec_dev(N_SEC - 1, 0))
     late = pass_along(0, c_kv)
     c_grad = spread(1, summed(0, 1, c_grad))
     late = pass_across(0, c_kv, late)
+    c_down = slices_send(0, glt, gsl)
+    c_hid = share_rest(hall, 0, HIDDEN_X_FIRST, c_hid)
     received(c_grad)
     grads_in(0, xs, 1)
+    c_total = sender.start(
+        fl.at[TL, mine, :], rx.at[2, mine, :], sec_dev(N_SEC - 1, 0)
+    )
+    c_low = section_spread(1, c_low)
     c_dkv = attend(0, c_kv, late)
     c_att = attention_out(0)
     c_dkv = attention_relay(0, c_dkv)
     c_up = send_section(0, xs[0, mine, :] - summed(0, 2, c_att))
-    c_low = sender.start(snd.at[0, 0], rx.at[1], sec_dev(N_SEC - 1, 0))
-    c_total = sender.start(fl.at[TL, pl.ds(0, rows), :], rx.at[2], sec_dev(N_SEC - 1, 0))
-    c_down = share_pass(hall, 0, HIDDEN_X_FIRST, c_hid) + slices_out(0, GL, glt, gsl)
+    c_down += share_pass(hall, 0, HIDDEN_X_FIRST, c_hid)
 
     is_last = sec == N_SEC - 1
     loads[11].wait()
@@ -591,39 +645,44 @@
     mlp_hidden(1)
     mlp_down(1)
     c_mlp = scatter(1, 0)
-    c_hid = share(hall, 1, HIDDEN_X_FIRST)
+    c_hid = share_rest(hall, 1, HIDDEN_X_FIRST, share(hall, 1, HIDDEN_X_FIRST))
     grad = summed(0, 3, c_att)
     c_gl = send_section(1, xs[3, mine, :] + norm_back(grad, slope, xs[1, mine, :]))
     c_mlp = spread(2, summed(1, 0, c_mlp))
-    received([c_low])
+    received(c_low)
     choose(1)
-    received(c_mlp)
-    c_kv = attention_in(1, hd, 2)
-    emit(1)
     received(c_gl)
     choose(3)
     mlp_back(1, hd)
     c_grad = scatter(1, 1)
+    received(c_mlp)
+    c_kv = attention_in(1, hd, 2)
+    emit(1)
+    c_total = section_spread(2, c_total)
+    grads_mlp()
+    c_grad = spread(3, summed(1, 1, c_grad))
     late = pass_along(1, c_kv)
-    c_gm = grads_mlp()
+    slices_out(1, GL, glt, gsl)
     late = pass_across(1, c_kv, late)
-    c_grad = spread(3, summed(1, 1, c_grad))
-    received([c_total])
+    red_m.first()
+    received(c_total)
     choose(2)
-    c_down += slices_out(1, GL, glt, gsl)
-    c_down += share_pass(hall, 1, HIDDEN_X_FIRST, c_hid)
     received(c_grad)
     grads_in(1, hd, 3)
     emit(2)
     c_dkv = attend(1, c_kv, late)
     c_att = attention_out(1)
+    red_m.second_b()
+    c_down += share_pass(hall, 1, HIDDEN_X_FIRST, c_hid)
     c_dkv = attention_relay(1, c_dkv)
-    c_gm = reduce_second(gmlp, cut_mlp, ra_m, rb_m, rz_m, rw_m, c_gm)
-    c_ga = grads_att()
+    red_m.second_a()
+    grads_att()
     c_up = spread(4, summed(1, 2, c_att))
     c_att = attention_back(1, c_dkv)
-    c_gk = grads_kv()
+    grads_kv()
+    c_down += slices_send(1, glt, gsl)
     c_gl = spread(5, summed(1, 3, c_att))
+    red_m.third()
     received(c_up)
 
     def upper(r):
@@ -635,28 +694,27 @@
     copy = pltpu.make_async_copy(pre, recon_h.at[0], out_sem.at[0])
     copy.start()
     outs.append(copy)
+    red_a.second_b()
+    red_a.second_a()
     received(c_gl)
 
     def lower(r):
         here = pl.ds(r, 32)
-        hd[3, here, :] = hd[3, here, :] + norm_back(
-            ag[5, here, :].astype(F32), slope, xs_low(here)
-        )
-
-    def xs_low(here):
-        return hd[1, here, :]
+        hd[3, here, :] = hd[3, here, :] + norm_back(ag[5, here, :].astype(F32), slope, hd[1, here, :])
 
     loop(rows // 32, 32, lower)
     emit(3)
-    c_ga = reduce_second(gatt, cut_att, ra_a, rb_a, rz_a, rw_a, c_ga)
+    red_k.second_b()
+    red_k.second_a()
+    red_a.third()
     grads_down(c_down)
     finish(om.at[1], gdn_h, 5)
-    reduce_last(gmlp, cut_mlp, rz_m, rw_m, store_mlp, c_gm)
+    red_m.last(store_mlp)
     finish(om.at[0], gup_h, 4)
-    c_gk = reduce_second(gkv, cut_att, ra_k, rb_k, rz_k, rw_k, c_gk)
-    reduce_last(gatt, cut_att, rz_a, rw_a, store_qo, c_ga)
+    red_k.third()
+    red_a.last(store_qo)
     finish(oout, gout_h, 7)
-    reduce_last(gkv, cut_att, rz_k, rw_k, store_kv, c_gk)
+    red_k.last(store_kv)
     finish(oqkv, gqkv_h, 6)
     for copy in [c for c in sender.all if all(c is not f for f in c_first)]:
         copy.wait_send()
@@ -664,7 +722,7 @@
         copy.wait()
 
 
-N_COPIES = 312
+N_COPIES = 320
 
 
 def per_device(streams, head_streams, gains, w_qkv, w_out, w_up, w_down):
@@ -675,8 +733,8 @@
     heads = local // HEAD_DIM
     chunk = width // N_SEQ
     half = width // 2
-    cut_mlp = 768
-    cut_att = 384
+    cut_mlp = 512
+    cut_att = 256
     wqkv = jnp.transpose(w_qkv[0], (1, 2, 0)).reshape(3, heads, HEAD_DIM, width)
     wout = jnp.transpose(w_out[0], (1, 0)).reshape(heads, HEAD_DIM, width)
     sizes = (rows, width, hid, att, cut_mlp, cut_att)
@@ -684,6 +742,13 @@
     rest_m, rest_a = hid - cut_mlp, att - cut_att
     n_dx, n_dz = DKV_X_FIRST, heads - DKV_X_FIRST
     vm = pltpu.VMEM
+
+    def ring_buffers(left, right):
+        return (
+            vm((half, left), BF16), vm((2, 1, chunk // 2, left), BF16), vm((2, 1, chunk, left), BF16),
+            vm((2, 2, chunk // 2, right), BF16), vm((2, 2, chunk, right), BF16), vm((chunk, right), BF16),
+        )
+
     scratch = [
         vm((4, rows, width), F32), vm((4, rows, width), F32), vm((2, width), F32),
         vm((heads, 2, HEAD_DIM, width), BF16), vm((heads, 2, HEAD_DIM, width), BF16),
@@ -699,12 +764,7 @@
         vm((rows, hid), F32), vm((2 * rows, att), BF16),
         vm((N_SEQ * rows, 2 * rows), F32), vm((N_SEQ * rows, 2 * rows), BF16),
         vm((width, hid), BF16), vm((width, att), BF16), vm((width, att), BF16),
-        vm((half, cut_mlp), BF16), vm((N_Z - 1, chunk, cut_mlp), BF16),
-        vm((N_Z - 1, 2, chunk, rest_m), BF16), vm((chunk, rest_m), BF16),
-        vm((half, cut_att), BF16), vm((N_Z - 1, chunk, cut_att), BF16),
-        vm((N_Z - 1, 2, chunk, rest_a), BF16), vm((chunk, rest_a), BF16),
-        vm((half, cut_att), BF16), vm((N_Z - 1, chunk, cut_att), BF16),
-        vm((N_Z - 1, 2, chunk, rest_a), BF16), vm((chunk, rest_a), BF16),
+        *ring_buffers(cut_mlp, rest_m), *ring_buffers(cut_att, rest_a), *ring_buffers(cut_att, rest_a),
         vm((2, chunk, hid), BF16), vm((3, chunk, local), BF16), vm((chunk, local), BF16),
         pltpu.SemaphoreType.DMA((12,)), pltpu.SemaphoreType.DMA((8,)),
         pltpu.SemaphoreType.DMA((N_COPIES,)), pltpu.SemaphoreType.DMA((N_COPIES,)),

time: 191 us -> 174 us (0.911)
  Pallas kernels: 184 us -> 167 us
    pallas_call x1, Pallas kernels: 184 us -> 167 us  [per_device(): pl.pallas_call(lambda *refs: kernel(sizes, *refs), out_shape=(jax.ShapeDt...]
where the time goes in v4:
time: 174 us
  Pallas kernels  167 us (96%)
  local copies, waits for them, and re-layouts  6.49 us (4%)
    pallas_call x1, Pallas kernels, per_device(): pl.pallas_call(lambda *refs: kernel(sizes, *refs), out_shape=(jax.ShapeDt...  167 us
    unnamed x13, local copies, waits for them, and re-layouts  6.49 us

profile of v4, /device:TPU:1, one launch (start us, length us, event | category | flops | bytes accessed | tf_op | source)
XLA Modules:
  0.0 174.2 jit_solution(7042787487734217727)
XLA Ops:
  0.6 167.0 %window.1 = (f32[4,128,1280]{2,1,0:T(8,128)}, bf16[3,160,320]{2,1,0:T(8,128)(2,1)}, bf16[160,320]{1,0:T(8,128)(2,1)}, bf16[160,1280]{1,0:T(8,128)(2,1)}, bf16[160,1280]{1,0:T(8,128)(2,1)}) custom-call(f32[4,128,1280]{2,1,0:T(8,128)} %bitcast.23, f32[4,128,1280]{2,1,0:T(8,128)} %refs_1_.1, f32[2,1280]{1,0:T(2,128)} %bitcast.31, ...), custom_call_target="tpu_custom_call" | custom-call | tf_op jit(solution)/shard_map/window/pallas_call | solution.py:773
  167.7 0.0 copy-start.2
  167.7 0.0 copy-start.3
  167.7 0.0 copy-start.1
  167.7 0.0 copy-start
  167.7 3.6 %copy.17 = f32[1,4,128,1280]{3,2,1,0:T(8,128)} copy(f32[1,4,128,1280]{3,2,1,0:T(8,128)} %bitcast.24) | data formatting | bytes 5242880
  171.3 0.0 copy-done.2
  171.3 0.7 copy.18
  172.0 0.0 copy-done.3
  172.0 0.6 copy.19
  172.7 0.0 copy-done.1
  172.7 0.8 copy.20
  173.4 0.0 copy-done
  173.4 0.8 copy.21
Async XLA Ops:
  167.7 3.6 %copy-start.2 = (bf16[3,160,320]{2,1,0:T(8,128)(2,1)S(1)}, bf16[3,160,320]{2,1,0:T(8,128)(2,1)}, u32[]{:S(2)}) copy-start(bf16[3,160,320]{2,1,0:T(8,128)(2,1)} %get-tuple-element.11) | copy-start | bytes 921604
  167.7 4.4 %copy-start.3 = (bf16[160,320]{1,0:T(8,128)(2,1)S(1)}, bf16[160,320]{1,0:T(8,128)(2,1)}, u32[]{:S(2)}) copy-start(bf16[160,320]{1,0:T(8,128)(2,1)} %get-tuple-element.12) | copy-start | bytes 307204
  167.7 5.0 %copy-start.1 = (bf16[160,1280]{1,0:T(8,128)(2,1)S(1)}, bf16[160,1280]{1,0:T(8,128)(2,1)}, u32[]{:S(2)}) copy-start(bf16[160,1280]{1,0:T(8,128)(2,1)} %get-tuple-element.13) | copy-start | bytes 1228804
  167.7 5.7 %copy-start = (bf16[160,1280]{1,0:T(8,128)(2,1)S(1)}, bf16[160,1280]{1,0:T(8,128)(2,1)}, u32[]{:S(2)}) copy-start(bf16[160,1280]{1,0:T(8,128)(2,1)} %get-tuple-element.14) | copy-start | bytes 1228804

commit v5 on v4

--- a/solution.py
+++ b/solution.py
@@ -18,7 +18,7 @@
 N_SEC = 4
 KV_X_FIRST = 2
 DKV_X_FIRST = 3
-HIDDEN_X_FIRST = 768
+HIDDEN_X_FIRST = 1024
 NU, GL, AL, TL = 0, 1, 2, 3
 NN = (((1,), (0,)), ((), ()))
 NT = (((1,), (1,)), ((), ()))
@@ -362,13 +362,28 @@
             kv = kvb[t, h].reshape(tokens, PAIR)
             both = qd[:, lanes]
             scores[...] = dot(kv, both, NT)
-            logits = scores[:, :rows]
-            weight = jnp.exp(logits - jnp.max(logits, 0, keepdims=True))
-            probs = weight * (1.0 / jnp.sum(weight, 0, keepdims=True))
-            grad_probs = scores[:, rows:]
-            delta = jnp.sum(probs * grad_probs, 0, keepdims=True)
-            pd[:, rows:] = probs.astype(BF16)
-            pd[:, :rows] = (probs * (grad_probs - delta)).astype(BF16)
+            steps = [pl.ds(c * rows, rows) for c in range(N_SEQ)]
+
+            def folded(value, op):
+                return op(value.reshape(rows // 8, 8, rows), 0)
+
+            top = folded(scores[steps[0], :rows], jnp.max)
+            for here in steps[1:]:
+                top = jnp.maximum(top, folded(scores[here, :rows], jnp.max))
+            top = jnp.max(top, 0, keepdims=True)
+            total = jnp.zeros((8, rows), F32)
+            delta = jnp.zeros((8, rows), F32)
+            for here in steps:
+                weight = jnp.exp(scores[here, :rows] - top)
+                scores[here, :rows] = weight
+                total = total + folded(weight, jnp.sum)
+                delta = delta + folded(weight * scores[here, rows:], jnp.sum)
+            scale = 1.0 / jnp.sum(total, 0, keepdims=True)
+            delta = jnp.sum(delta, 0, keepdims=True) * scale
+            for here in steps:
+                probs = scores[here, :rows] * scale
+                pd[here, rows:] = probs.astype(BF16)
+                pd[here, :rows] = (probs * (scores[here, rows:] - delta)).astype(BF16)
             dks[t, h] = dot(pd[...], both, NN).astype(BF16).reshape(2, N_Z, rows, PAIR)
             if h < DKV_X_FIRST:
                 first.append([sender.start(dks.at[t, h, 1], dax.at[t, h], seq_dev(N_Z))])

time: 174 us -> 177 us (1.017)
  Pallas kernels: 167 us -> 169 us
    pallas_call x1, Pallas kernels: 167 us -> 169 us  [per_device(): pl.pallas_call(lambda *refs: kernel(sizes, *refs), out_shape=(jax.ShapeDt...]
where the time goes in v5:
time: 177 us
  Pallas kernels  169 us (95%)
  local copies, waits for them, and re-layouts  6.49 us (4%)
    pallas_call x1, Pallas kernels, per_device(): pl.pallas_call(lambda *refs: kernel(sizes, *refs), out_shape=(jax.ShapeDt...  169 us
    unnamed x13, local copies, waits for them, and re-layouts  6.49 us

profile of v5, /device:TPU:1, one launch (start us, length us, event | category | flops | bytes accessed | tf_op | source)
XLA Modules:
  0.0 176.6 jit_solution(723495271053451955)
XLA Ops:
  0.6 169.4 %window.1 = (f32[4,128,1280]{2,1,0:T(8,128)}, bf16[3,160,320]{2,1,0:T(8,128)(2,1)}, bf16[160,320]{1,0:T(8,128)(2,1)}, bf16[160,1280]{1,0:T(8,128)(2,1)}, bf16[160,1280]{1,0:T(8,128)(2,1)}) custom-call(f32[4,128,1280]{2,1,0:T(8,128)} %bitcast.23, f32[4,128,1280]{2,1,0:T(8,128)} %refs_1_.1, f32[2,1280]{1,0:T(2,128)} %bitcast.31, ...), custom_call_target="tpu_custom_call" | custom-call | tf_op jit(solution)/shard_map/window/pallas_call | solution.py:788
  170.1 0.0 copy-start.2
  170.1 0.0 copy-start.3
  170.1 0.0 copy-start.1
  170.1 0.0 copy-start
  170.1 3.6 %copy.17 = f32[1,4,128,1280]{3,2,1,0:T(8,128)} copy(f32[1,4,128,1280]{3,2,1,0:T(8,128)} %bitcast.24) | data formatting | bytes 5242880
  173.7 0.0 copy-done.2
  173.7 0.7 copy.18
  174.4 0.0 copy-done.3
  174.4 0.6 copy.19
  175.1 0.0 copy-done.1
  175.1 0.8 copy.20
  175.8 0.0 copy-done
  175.8 0.8 copy.21
Async XLA Ops:
  170.1 3.6 %copy-start.2 = (bf16[3,160,320]{2,1,0:T(8,128)(2,1)S(1)}, bf16[3,160,320]{2,1,0:T(8,128)(2,1)}, u32[]{:S(2)}) copy-start(bf16[3,160,320]{2,1,0:T(8,128)(2,1)} %get-tuple-element.11) | copy-start | bytes 921604
  170.1 4.4 %copy-start.3 = (bf16[160,320]{1,0:T(8,128)(2,1)S(1)}, bf16[160,320]{1,0:T(8,128)(2,1)}, u32[]{:S(2)}) copy-start(bf16[160,320]{1,0:T(8,128)(2,1)} %get-tuple-element.12) | copy-start | bytes 307204
  170.1 5.0 %copy-start.1 = (bf16[160,1280]{1,0:T(8,128)(2,1)S(1)}, bf16[160,1280]{1,0:T(8,128)(2,1)}, u32[]{:S(2)}) copy-start(bf16[160,1280]{1,0:T(8,128)(2,1)} %get-tuple-element.13) | copy-start | bytes 1228804
  170.1 5.7 %copy-start = (bf16[160,1280]{1,0:T(8,128)(2,1)S(1)}, bf16[160,1280]{1,0:T(8,128)(2,1)}, u32[]{:S(2)}) copy-start(bf16[160,1280]{1,0:T(8,128)(2,1)} %get-tuple-element.14) | copy-start | bytes 1228804
